TPU v7x, 32 devices: a whole 2x2x4 slice. The times are simulated.
32 devices in a mesh: wide: 8 (over z, y), narrow: 4 (over x, core).
Axes of the slice: x: 2, y: 2, z: 4, core: 2. Of those that a mesh axis runs over, the one named last changes fastest.
Arguments:
- density_blocks: float32 [768, 128, 128], P(('wide', 'narrow')), may hold values from -0.4 to 0.4
- block_groups: int32 [768, 2], P(('wide', 'narrow')), may hold values from 0 to 63
- block_brick: int32 [768], P(('wide', 'narrow')), may hold values from 0 to 8191, as said below
- orbital_freq: float32 [3, 8192], replicated, may hold values from 0.1 to 2
- orbital_phase: float32 [3, 8192], replicated, may hold values from -3.140625 to 3.140625
- core_density: float32 [8, 1024, 1024], P('wide', None, 'narrow'), may hold values from 0.2 to 2
Outputs:
- xc_spectrum: float32 [8, 2, 1024, 512], P('wide', None, 'narrow')
Inputs may be any that keep to these rules, and one draw needn't show every extreme that they name: `block_brick`: every block stored on the device of narrow index n has its brick within the columns n * 1024 / 4 to (n + 1) * 1024 / 4 - 1 of the grid. The blocks of one device have at most 6 bricks, counted with repeats, in the planes of any one index of wide, and some device has exactly 6.
All inputs are finite; a program needn't handle non-finite values.
Results may differ from a plain program's by a relative error of at most 0.0003.
Values sent between devices are 32-bit elements; how exact they have to be, the bound alone decides.
No kernel may reach another device: no remote copies, remote signals or barrier semaphores. Data moves between devices by JAX's collectives and lax.ppermute only.
A program may use at most 64 MiB of HBM per device.

v0:
```python
import functools
import math

import jax
import jax.numpy as jnp
from jax import lax
from jax.experimental import pallas as pl
from jax.experimental.pallas import tpu as pltpu
from jax.sharding import PartitionSpec as P

NX = 1024
NY = 1024
GRP = 128
BY = 32
BX = 32
LANES = 128
SUB = 8

f32 = jnp.float32
bf16 = jnp.bfloat16
i32 = jnp.int32

energy_coef = -0.75 * (3.0 / math.pi) ** (1.0 / 3.0)

COS_FIT = (0.999999989, -0.499999891, 0.0416664892, -0.00138878036, 2.47698836e-05, -2.70790308e-07, 1.72450917e-09)
SIN_FIT = (0.999999999, -0.166666659, 0.00833332129, -0.000198405341, 2.753585e-06, -2.47288117e-08, 1.36130988e-10)
TURN_HI = 6.28125
TURN_LO = 2.0 * math.pi - TURN_HI


def horner(w, fit):
    total = jnp.full_like(w, fit[-1])
    for term in fit[-2::-1]:
        total = total * w + term
    return total


def cos_any(angle):
    turns = jnp.floor(angle * (0.5 / math.pi) + 0.5)
    r = (angle - turns * TURN_HI) - turns * TURN_LO
    return horner(r * r, COS_FIT)


def cos_sin_turn(step, length):
    r = (step - length // 2).astype(f32) * (2.0 * math.pi / length)
    w = r * r
    return -horner(w, COS_FIT), -(r * horner(w, SIN_FIT))


def split(value):
    high = value.astype(bf16)
    return high, (value - high.astype(f32)).astype(bf16)


def dot3(lhs_high, lhs_low, rhs_high, rhs_low):
    dot = functools.partial(jnp.dot, preferred_element_type=f32)
    return dot(lhs_high, rhs_high) + dot(lhs_low, rhs_high) + dot(lhs_high, rhs_low)


def pieces_kernel(
    steps, per_step, slots, planes, groups_ref, brick_ref, blocks_ref, freq_ref, phase_ref,
    send_ref, count_ref, left_ref, right_ref, mixed_ref,
):
    row_bricks = NX // BX
    col_bricks = NY // BY
    wide_size = send_ref.shape[0]
    narrow_size = lax.axis_size("narrow")
    narrow = lax.axis_index("narrow")
    column_bricks = row_bricks // narrow_size
    flip = (2 * narrow < narrow_size).astype(i32)
    step = pl.program_id(0)
    lane = lax.broadcasted_iota(i32, (SUB, LANES), 1)
    row = lax.broadcasted_iota(i32, (BY, GRP), 0)

    @pl.when(step == 0)
    def _():
        zero = jnp.zeros((slots * SUB, LANES), f32)
        none = jnp.full((SUB, LANES), -1.0, f32)
        for w in range(wide_size):
            send_ref[w, : slots * SUB, :] = zero
            send_ref[w, slots * SUB :, :] = none
            count_ref[w] = 0

    def one_block(k, carry):
        b = step * per_step + k
        q = brick_ref[b]
        xb = q % row_bricks
        yb = (q // row_bricks) % col_bricks
        zb = q // (row_bricks * col_bricks)
        home = zb // planes
        local = ((zb % planes) * col_bricks + yb) * column_bricks + (xb - narrow * column_bricks)
        rank = count_ref[home]
        count_ref[home] = rank + 1

        ys = (yb * BY + row).astype(f32)
        xs = (xb * BX + jnp.where(flip == 1, BX - 1 - row, row)).astype(f32)
        zs = zb.astype(f32)

        def factors(side):
            group = groups_ref[side, b]
            at = pl.ds(pl.multiple_of(group * GRP, GRP), GRP)
            freq = freq_ref[:, at]
            phase = phase_ref[:, at]
            along_x = cos_any(xs * freq[0:1] + phase[0:1])
            along_y = cos_any(ys * freq[1:2] + phase[1:2])
            along_z = cos_any(jnp.broadcast_to(zs * freq[2:3] + phase[2:3], (SUB, GRP)))
            return along_x, along_y * along_z[0:1]

        left_x, left_y = factors(0)
        right_x, right_y = factors(1)
        left = (left_x[None, :, None, :] * left_y.reshape(BY // SUB, 1, SUB, GRP)).reshape(BY * BX, GRP)
        high, low = split(left)
        left_ref[:, :GRP] = high
        left_ref[:, GRP:] = low
        d_high, d_low = split(blocks_ref[k])
        right_ref[:GRP, :GRP] = d_high
        right_ref[GRP:, :GRP] = d_high
        right_ref[:GRP, GRP:] = d_low
        right_ref[GRP:, GRP:] = d_low
        mixed_ref[...] = jnp.dot(left_ref[...], right_ref[...], preferred_element_type=f32)

        def merge(value, bit):
            count = value.shape[0]
            pair = value.reshape(count // 2, 2, SUB, LANES)
            first, second = pair[:, 0], pair[:, 1]
            odd = (lane & bit) != 0
            keep = jnp.where(odd, second, first)
            move = jnp.where(odd, first, second)
            moved = pltpu.roll(move.reshape(-1, LANES), bit, 1).reshape(count // 2, SUB, LANES)
            return keep + moved

        parts = []
        for chunk in range(8):
            rows = pl.ds(chunk * 128, 128)
            mixed = mixed_ref[rows, :GRP] + mixed_ref[rows, GRP:]
            g, x0 = chunk // 2, (chunk % 2) * 16
            right = right_x[x0 : x0 + 16][:, None, :] * right_y[g * SUB : (g + 1) * SUB][None]
            value = mixed.reshape(16, SUB, GRP) * right
            for bit in (1, 2, 4, 8):
                value = merge(value, bit)
            parts.append(value)
        value = jnp.concatenate(parts, axis=0)
        for bit in (16, 32, 64):
            value = merge(value, bit)
        at = pl.multiple_of(rank * SUB, SUB)
        send_ref[home, pl.ds(at, SUB), :] = value[0]
        send_ref[home, pl.ds(slots * SUB + rank, 1), :] = jnp.full((1, LANES), 1.0, f32) * local.astype(f32)
        return carry

    lax.fori_loop(0, per_step, one_block, 0)


def make_pieces(blocks, groups, bricks, freq, phase, wide_size, slots, planes):
    count = blocks.shape[0]
    per_step = math.gcd(count, 8)
    steps = count // per_step
    rows = slots * SUB + SUB
    return pl.pallas_call(
        functools.partial(pieces_kernel, steps, per_step, slots, planes),
        grid=(steps,),
        in_specs=[
            pl.BlockSpec(memory_space=pltpu.SMEM),
            pl.BlockSpec(memory_space=pltpu.SMEM),
            pl.BlockSpec((per_step, GRP, GRP), lambda s: (s, 0, 0)),
            pl.BlockSpec(freq.shape, lambda s: (0, 0)),
            pl.BlockSpec(phase.shape, lambda s: (0, 0)),
        ],
        out_specs=pl.BlockSpec((wide_size, rows, LANES), lambda s: (0, 0, 0)),
        out_shape=jax.ShapeDtypeStruct((wide_size, rows, LANES), f32),
        scratch_shapes=[
            pltpu.SMEM((wide_size,), i32),
            pltpu.VMEM((BY * BX, 2 * GRP), bf16),
            pltpu.VMEM((2 * GRP, 2 * GRP), bf16),
            pltpu.VMEM((BY * BX, 2 * GRP), f32),
        ],
        name="pieces",
    )(groups.T, bricks, blocks, freq, phase)


def energy_kernel(slots, ids_ref, got_ref, core_ref, out_ref, first_ref, valence_ref, cells_ref):
    wide_size = got_ref.shape[0]
    total = wide_size * slots
    narrow_size = lax.axis_size("narrow")
    narrow = lax.axis_index("narrow")
    column_bricks = core_ref.shape[1] // BX
    tiles = LANES // BX
    flip = 2 * narrow < narrow_size
    lane = lax.broadcasted_iota(i32, (SUB, LANES), 1)
    group = lane // BX

    for s in range(total - 1, -1, -1):
        first_ref[jnp.maximum(ids_ref[s], 0)] = s
    for s in range(total):
        valence_ref[s * SUB : (s + 1) * SUB, :] = got_ref[s // slots, (s % slots) * SUB : (s % slots + 1) * SUB, :]
    head = jnp.full((SUB, LANES), -1.0, f32)
    sub = lax.broadcasted_iota(i32, (SUB, LANES), 0)
    for s in range(total):
        brick = ids_ref[s]
        at = jnp.maximum(brick, 0)
        valid = brick >= 0
        owner = first_ref[at]

        @pl.when(owner != s)
        def _():
            rows = pl.ds(pl.multiple_of(owner * SUB, SUB), SUB)
            valence_ref[rows, :] = valence_ref[rows, :] + got_ref[s // slots, (s % slots) * SUB : (s % slots + 1) * SUB, :]

        column = at % column_bricks
        placed = jnp.where(flip, at - column + (column_bricks - 1 - column), at)
        mark = jnp.where(owner == s, placed, -1).astype(f32)
        head = jnp.where((lane == s % LANES) & (sub == s // LANES), mark, head)
        y0 = pl.multiple_of((at // column_bricks) * BY, BY)
        lanes = pl.ds(pl.multiple_of((column // tiles) * LANES, LANES), LANES)
        block = core_ref[pl.ds(y0, BY), lanes]
        block = pltpu.roll(block, ((tiles - column % tiles) % tiles) * BX, 1)
        value = block[0:SUB]
        for g in range(1, tiles):
            moved = pltpu.roll(block[g * SUB : (g + 1) * SUB], g * BX, 1)
            value = jnp.where(group == g, moved, value)
        cells_ref[s * SUB : (s + 1) * SUB, :] = value

    core = cells_ref[...]
    source = lax.broadcasted_iota(i32, (LANES, LANES), 0)
    target = lax.broadcasted_iota(i32, (LANES, LANES), 1)
    wanted = jnp.where(flip, (target // BX) * BX + (BX - 1 - target % BX), target)
    shuffle = (source == wanted).astype(bf16)
    high = core.astype(bf16)
    rest = core - high.astype(f32)
    mid = rest.astype(bf16)
    low = (rest - mid.astype(f32)).astype(bf16)
    dot = functools.partial(jnp.dot, preferred_element_type=f32)
    core = (dot(low, shuffle) + dot(mid, shuffle)) + dot(high, shuffle)

    def four_thirds(value):
        size = jnp.maximum(jnp.abs(value), 1e-30)
        inverse = jnp.exp2(jnp.log2(size) * (-1.0 / 3.0))
        inverse = inverse * (4.0 - size * (inverse * inverse * inverse)) * (1.0 / 3.0)
        return size * (size * (inverse * inverse))

    rho = core + valence_ref[...]
    out_ref[: total * SUB, :] = energy_coef * (four_thirds(rho) - four_thirds(core))
    out_ref[total * SUB :, :] = head


def make_energy(got, ids, core, slots):
    wide_size = got.shape[0]
    total = wide_size * slots
    bricks = (core.shape[0] // BY) * (core.shape[1] // BX)
    return pl.pallas_call(
        functools.partial(energy_kernel, slots),
        in_specs=[
            pl.BlockSpec(memory_space=pltpu.SMEM),
            pl.BlockSpec(memory_space=pltpu.VMEM),
            pl.BlockSpec(memory_space=pltpu.VMEM),
        ],
        out_specs=pl.BlockSpec(memory_space=pltpu.VMEM),
        out_shape=jax.ShapeDtypeStruct(((total + 1) * SUB, LANES), f32),
        scratch_shapes=[
            pltpu.SMEM((bricks,), i32),
            pltpu.VMEM((total * SUB, LANES), f32),
            pltpu.VMEM((total * SUB, LANES), f32),
        ],
        name="energy",
    )(ids, got, core)


def tables_kernel(wy_high, wy_low, wx_high, wx_low):
    rows_all = NY // lax.axis_size("narrow")
    narrow = lax.axis_index("narrow")
    half = rows_all // 2
    depth = NY // 2
    lane = lax.broadcasted_iota(i32, (half, LANES), 1)
    row = lax.broadcasted_iota(i32, (half, LANES), 0)
    for p in range(2):
        wave = rows_all * narrow + 2 * row + p
        base_cos, base_sin = cos_sin_turn((wave * lane) % NY, NY)
        for t in range(depth // LANES):
            jump_cos, jump_sin = cos_sin_turn((wave[:SUB] * (t * LANES)) % NY, NY)
            jump_cos = jnp.concatenate([jump_cos] * (half // SUB), axis=0)
            jump_sin = jnp.concatenate([jump_sin] * (half // SUB), axis=0)
            at = slice(t * LANES, (t + 1) * LANES)
            for part, value in (
                (0, base_cos * jump_cos - base_sin * jump_sin),
                (1, -(base_sin * jump_cos + base_cos * jump_sin)),
            ):
                rows = slice(p * rows_all + part * half, p * rows_all + (part + 1) * half)
                wy_high[rows, at], wy_low[rows, at] = split(value)
    depth = NX // 2
    lane = lax.broadcasted_iota(i32, (depth, LANES), 1)
    place = 2 * lax.broadcasted_iota(i32, (depth, LANES), 0) + 1
    base_cos, base_sin = cos_sin_turn((place * lane) % (2 * NX), 2 * NX)
    for t in range(NX // 2 // LANES):
        jump_cos, jump_sin = cos_sin_turn((place[:SUB] * (t * LANES)) % (2 * NX), 2 * NX)
        jump_cos = jnp.concatenate([jump_cos] * (depth // SUB), axis=0)
        jump_sin = jnp.concatenate([jump_sin] * (depth // SUB), axis=0)
        at = slice(t * LANES, (t + 1) * LANES)
        for part, value in (
            (0, base_cos * jump_cos - base_sin * jump_sin),
            (1, base_sin * jump_cos + base_cos * jump_sin),
        ):
            rows = slice(part * depth, (part + 1) * depth)
            wx_high[rows, at], wx_low[rows, at] = split(value)


def make_tables(narrow_size):
    rows_all = NY // narrow_size
    y_shape = jax.ShapeDtypeStruct((2 * rows_all, NY // 2), bf16)
    x_shape = jax.ShapeDtypeStruct((NX, NX // 2), bf16)
    vmem = pl.BlockSpec(memory_space=pltpu.VMEM)
    return pl.pallas_call(
        tables_kernel,
        out_specs=[vmem] * 4,
        out_shape=[y_shape, y_shape, x_shape, x_shape],
        name="tables",
    )()


def along_y(total, ids_ref, bricks_ref, wy_high, wy_low, plane_ref, out_ref):
    columns = plane_ref.shape[1]
    column_bricks = columns // BX
    tiles = LANES // BX
    lane = lax.broadcasted_iota(i32, (SUB, LANES), 1)
    group = lane // BX
    plane_ref[...] = jnp.zeros(plane_ref.shape, f32)
    for s in range(total):
        brick = ids_ref[s]
        valid = brick >= 0
        at = jnp.maximum(brick, 0)
        column = at % column_bricks
        y0 = jnp.where(valid, (at // column_bricks) * BY, NY)
        lanes = pl.ds(pl.multiple_of((column // tiles) * LANES, LANES), LANES)
        value = pltpu.roll(bricks_ref[s * SUB : (s + 1) * SUB, :], (column % tiles) * BX, 1)
        mask = group == column % tiles
        for g in range(tiles):
            moved = value if g == 0 else pltpu.roll(value, LANES - g * BX, 1)
            rows = pl.ds(pl.multiple_of(y0 + g * SUB, SUB), SUB)
            pltpu.store(plane_ref.at[rows, lanes], moved, mask=mask)
    half = NY // 2
    rows_all = wy_high.shape[0] // 2
    upper = plane_ref[:half, :]
    lower = plane_ref[half:NY, :]
    for p in range(2):
        high, low = split(upper + lower if p == 0 else upper - lower)
        rows = slice(p * rows_all, (p + 1) * rows_all)
        value = dot3(wy_high[rows, :], wy_low[rows, :], high, low)
        for part in range(2):
            for t in range(columns // LANES):
                piece = value[part * rows_all // 2 : (part + 1) * rows_all // 2, t * LANES : (t + 1) * LANES]
                out_ref[part, t, pl.ds(p, rows_all // 2, stride=2), :] = piece


def y_kernel(total, ids_ref, bricks_ref, wy_high, wy_low, out_ref, plane_ref):
    along_y(total, ids_ref, bricks_ref, wy_high, wy_low, plane_ref, out_ref)


def make_y(ids, bricks, tables, columns):
    total = ids.shape[0]
    vmem = pl.BlockSpec(memory_space=pltpu.VMEM)
    return pl.pallas_call(
        functools.partial(y_kernel, total),
        in_specs=[pl.BlockSpec(memory_space=pltpu.SMEM), vmem, vmem, vmem],
        out_specs=vmem,
        out_shape=jax.ShapeDtypeStruct((2, columns // LANES, tables[0].shape[0] // 2, LANES), f32),
        scratch_shapes=[pltpu.VMEM((NY + BY, columns), f32)],
        cost_estimate=pl.CostEstimate(flops=2 * 10**9, bytes_accessed=2 * 10**6, transcendentals=0),
        name="along_y",
    )(ids, bricks, tables[0], tables[1])


def x_kernel(total, half_size, *refs):
    late_refs, refs = refs[: 2 * half_size], refs[2 * half_size :]
    wy_high, wy_low, wx_high, wx_low = refs[:4]
    early_refs, out_ref, plane_ref = refs[4 : 4 + half_size], refs[4 + half_size], refs[5 + half_size]
    late_y_refs = refs[6 + half_size :]
    narrow_size = 2 * half_size
    narrow = lax.axis_index("narrow")
    tiles = early_refs[0].shape[1]
    columns = tiles * LANES
    for k in range(half_size):
        along_y(total, late_refs[2 * k], late_refs[2 * k + 1], wy_high, wy_low, plane_ref, late_y_refs[k])

    def whole(ref, part):
        return jnp.concatenate([ref[part, t] for t in range(tiles)], axis=1)

    u = v = None
    for mask in range(half_size):
        near_ref = early_refs[mask]
        far_ref = late_y_refs[half_size - 1 - mask]
        source = lax.bitwise_xor(narrow, mask)
        mirror = narrow_size - 1 - source
        sign = jnp.where(source < mirror, 1.0, -1.0).astype(f32)
        start = pl.multiple_of((jnp.maximum(source, mirror) - half_size) * columns, columns)
        cos_rows = pl.ds(start, columns)
        sin_rows = pl.ds(pl.multiple_of(NX // 2 + start, columns), columns)
        c = (wx_high[cos_rows, :], wx_low[cos_rows, :])
        s = (wx_high[sin_rows, :], wx_low[sin_rows, :])
        near = [whole(near_ref, part) for part in range(2)]
        far = [whole(far_ref, part) for part in range(2)]
        even = [split(a + b) for a, b in zip(near, far)]
        odd = [split((b - a) * sign) for a, b in zip(near, far)]
        u_new = dot3(*even[0], *c) + dot3(*odd[1], *s)
        v_new = dot3(*even[1], *c) - dot3(*odd[0], *s)
        u = u_new if u is None else u + u_new
        v = v_new if v is None else v + v_new
    lane = lax.broadcasted_iota(i32, (SUB, NX // 2), 1)
    phase_cos, phase_sin = cos_sin_turn((lane * (NX - 1)) % (2 * NX), 2 * NX)
    scale = 1.0 / math.sqrt(NX * NY)
    phase_cos, phase_sin = phase_cos[0:1] * scale, phase_sin[0:1] * scale
    out_ref[0] = u * phase_cos + v * phase_sin
    out_ref[1] = v * phase_cos - u * phase_sin


def make_x(late, tables, early):
    half_size = len(early)
    total = late[0][0].shape[0]
    rows_all = tables[0].shape[0] // 2
    columns = early[0].shape[1] * LANES
    vmem = pl.BlockSpec(memory_space=pltpu.VMEM)
    smem = pl.BlockSpec(memory_space=pltpu.SMEM)
    return pl.pallas_call(
        functools.partial(x_kernel, total, half_size),
        in_specs=[smem, vmem] * half_size + [vmem] * (4 + half_size),
        out_specs=vmem,
        out_shape=jax.ShapeDtypeStruct((2, rows_all, NX // 2), f32),
        scratch_shapes=[pltpu.VMEM((NY + BY, columns), f32)] + [pltpu.VMEM(early[0].shape, f32)] * half_size,
        name="along_x",
    )(*[part for pair in late for part in pair], *tables, *early)


def local(density_blocks, block_groups, block_brick, orbital_freq, orbital_phase, core_density):
    wide_size = lax.axis_size("wide")
    narrow_size = lax.axis_size("narrow")
    block_count = density_blocks.shape[0]
    slots = (2 * block_count + wide_size - 1) // wide_size
    planes, grid_rows, columns = core_density.shape
    half_size = narrow_size // 2
    assert narrow_size & (narrow_size - 1) == 0 and planes == 1 and slots <= SUB
    send = make_pieces(
        density_blocks, block_groups, block_brick, orbital_freq, orbital_phase, wide_size, slots, planes
    )
    got = lax.all_to_all(send, "wide", split_axis=0, concat_axis=0, tiled=True)
    total = wide_size * slots
    ids = got[:, slots * SUB : slots * SUB + slots, 0].astype(i32).reshape(total)
    own = make_energy(got, ids, core_density.reshape(grid_rows, columns), slots)

    def across(value, mask):
        return lax.ppermute(value, "narrow", [(i, i ^ mask) for i in range(narrow_size)])

    def ids_of(bricks):
        return bricks[total * SUB :].reshape(-1)[:total].astype(i32)

    bricks = {0: own}
    step = half_size
    while step:
        bricks |= {mask | step: across(value, step) for mask, value in bricks.items()}
        step //= 2
    tables = make_tables(narrow_size)
    early = [make_y(ids_of(bricks[mask]), bricks[mask], tables, columns) for mask in range(half_size)]
    late = [(ids_of(bricks[mask]), bricks[mask]) for mask in range(half_size, narrow_size)]
    return make_x(late, tables, early)[None]


def solution(mesh):
    return jax.shard_map(
        local,
        mesh=mesh,
        in_specs=(
            P(("wide", "narrow"), None, None),
            P(("wide", "narrow"), None),
            P(("wide", "narrow")),
            P(),
            P(),
            P("wide", None, "narrow"),
        ),
        out_specs=P("wide", None, "narrow", None),
        check_vma=False,
    )
```

profile of v0, /device:TPU:0, one launch (start us, length us, event | category | flops | bytes accessed | tf_op | source)
XLA Modules:
  0.0 68.5 jit_solution(11610161764770207886)
XLA Ops:
  0.0 22.1 %pieces.1 = f32[8,56,128]{2,1,0:T(8,128)} custom-call(s32[2,24]{1,0:T(2,128)} %bitcast.12, s32[24]{0:T(128)} %brick_ref.1, f32[24,128,128]{2,1,0:T(8,128)} %blocks_ref.1, f32[3,8192]{1,0:T(4,128)} %freq_ref.1, f32[3,8192]{1,0:T(4,128)} %phase_ref.1), custom_call_target="tpu_custom_call" | custom-call | tf_op jit(solution)/shard_map/pieces/pallas_call | solution.py:158
  22.1 7.3 %all-to-all-start = ((f32[8,56,128]{2,1,0:T(8,128)}), f32[8,56,128]{2,1,0:T(8,128)S(1)}, u32[]{:S(2)}, u32[]{:S(2)}) async-start(f32[8,56,128]{2,1,0:T(8,128)} %pieces.1), calls=%async_computation | async-start | bytes 458752 | tf_op jit(solution)/shard_map/all_to_all | solution.py:441
  29.4 2.8 %tables.1 = (bf16[512,512]{1,0:T(8,128)(2,1)}, bf16[512,512]{1,0:T(8,128)(2,1)}, bf16[1024,512]{1,0:T(8,128)(2,1)}, bf16[1024,512]{1,0:T(8,128)(2,1)}) custom-call(), custom_call_target="tpu_custom_call" | custom-call | tf_op jit(solution)/shard_map/tables/pallas_call | solution.py:310
  32.2 5.6 %all-to-all-done.got_ref = f32[8,56,128]{2,1,0:T(8,128)S(1)} async-done(((f32[8,56,128]{2,1,0:T(8,128)}), f32[8,56,128]{2,1,0:T(8,128)S(1)}, u32[]{:S(2)}, u32[]{:S(2)}) %all-to-all-start) | async-done | bytes 229408 | tf_op jit(solution)/shard_map/all_to_all | solution.py:441
  37.8 0.2 fusion
  38.0 0.6 convert_element_type.20.ids_ref
  38.6 0.0 copy-done
  38.6 9.2 %energy.1.bricks_ref = f32[392,128]{1,0:T(8,128)} custom-call(s32[48]{0:T(128)} %convert_element_type.20.ids_ref, f32[8,56,128]{2,1,0:T(8,128)} %copy-done, f32[1024,256]{1,0:T(8,128)} %bitcast.11), custom_call_target="tpu_custom_call" | custom-call | tf_op jit(solution)/shard_map/energy/pallas_call | solution.py:249
  47.9 0.7 slice_bitcast_fusion.1
  48.5 0.0 collective-permute-start.2
  48.5 1.5 %collective-permute-start = (f32[392,128]{1,0:T(8,128)}, f32[392,128]{1,0:T(8,128)S(1)}, u32[]{:S(2)}, u32[]{:S(2)}) collective-permute-start(f32[392,128]{1,0:T(8,128)} %energy.1.bricks_ref), channel_id=1, source_target_pairs={{0,2},{1,3},{2,0},{3,1},{4,6},{5,7},{6,4},{7,5},{8,10},{9,11},{10,... | collective-permute-start | bytes 602120 | tf_op jit(solution)/shard_map/ppermute | solution.py:447
  50.0 0.5 slice_convert_fusion.2.ids_ref
  50.5 3.5 %along_y.2.refs_8_ = f32[2,2,256,128]{3,2,1,0:T(8,128)} custom-call(s32[48]{0:T(128)} %slice_convert_fusion.2.ids_ref, f32[392,128]{1,0:T(8,128)} %energy.1.bricks_ref, bf16[512,512]{1,0:T(8,128)(2,1)} %get-tuple-element.9.wy_high.refs_4_, bf16[512,512]{1,0:T(8,128)(2,1)} %get-tuple-element.10.wy_low.refs_5_), custom_call_target="tpu_custom_call" | custom-call | flops 2000000000 | bytes 2000000 | tf_op jit(solution)/shard_map/along_y/pallas_call | solution.py:359
  54.1 0.0 collective-permute-done.2.bricks_ref
  54.1 0.6 slice_convert_fusion.1.ids_ref
  54.7 1.4 %collective-permute-done.refs_1_ = f32[392,128]{1,0:T(8,128)S(1)} collective-permute-done((f32[392,128]{1,0:T(8,128)}, f32[392,128]{1,0:T(8,128)S(1)}, u32[]{:S(2)}, u32[]{:S(2)}) %collective-permute-start) | collective-permute-done | bytes 200736 | tf_op jit(solution)/shard_map/ppermute | solution.py:447
  56.1 0.0 collective-permute-start.1
  56.1 0.6 slice_convert_fusion.4.refs_0_
  56.8 0.0 copy-done.3
  56.8 3.5 %along_y.3.refs_9_ = f32[2,2,256,128]{3,2,1,0:T(8,128)} custom-call(s32[48]{0:T(128)} %slice_convert_fusion.1.ids_ref, f32[392,128]{1,0:T(8,128)} %copy-done.3, bf16[512,512]{1,0:T(8,128)(2,1)} %get-tuple-element.9.wy_high.refs_4_, bf16[512,512]{1,0:T(8,128)(2,1)} %get-tuple-element.10.wy_low.refs_5_), custom_call_target="tpu_custom_call" | custom-call | flops 2000000000 | bytes 2000000 | tf_op jit(solution)/shard_map/along_y/pallas_call | solution.py:359
  60.3 0.0 collective-permute-done.1.refs_3_
  60.3 0.6 slice_convert_fusion.3.refs_2_
  60.9 0.1 copy-done.2
  61.0 7.5 %along_x.1 = f32[2,256,512]{2,1,0:T(8,128)} custom-call(s32[48]{0:T(128)} %slice_convert_fusion.4.refs_0_, f32[392,128]{1,0:T(8,128)} %copy-done.1, s32[48]{0:T(128)} %slice_convert_fusion.3.refs_2_, f32[392,128]{1,0:T(8,128)} %copy-done.2, bf16[512,512]{1,0:T(8,128)(2,1)} %get-tuple-element.9.wy_high.refs_4_, ...), custom_call_target="tpu_custom_call" | custom-call | tf_op jit(solution)/shard_map/along_x/pallas_call | solution.py:420
  (8 shorter events, 0.0 us)
Async XLA Ops:
  22.1 15.8 %all-to-all-start = ((f32[8,56,128]{2,1,0:T(8,128)}), f32[8,56,128]{2,1,0:T(8,128)S(1)}, u32[]{:S(2)}, u32[]{:S(2)}) async-start(f32[8,56,128]{2,1,0:T(8,128)} %pieces.1), calls=%async_computation | async-start | bytes 458752 | tf_op jit(solution)/shard_map/all_to_all | solution.py:441
  37.8 0.8 %copy-start = (f32[8,56,128]{2,1,0:T(8,128)}, f32[8,56,128]{2,1,0:T(8,128)S(1)}, u32[]{:S(2)}) copy-start(f32[8,56,128]{2,1,0:T(8,128)S(1)} %all-to-all-done.got_ref) | copy-start | bytes 688132
  48.5 5.5 %collective-permute-start.2 = (f32[392,128]{1,0:T(8,128)}, f32[392,128]{1,0:T(8,128)S(1)}, u32[]{:S(2)}, u32[]{:S(2)}) collective-permute-start(f32[392,128]{1,0:T(8,128)} %energy.1.bricks_ref), channel_id=1, source_target_pairs={{0,1},{1,0},{2,3},{3,2},{4,5},{5,4},{6,7},{7,6},{8,9},{9,8},{10,11... | collective-permute-start | bytes 602120 | tf_op jit(solution)/shard_map/ppermute | solution.py:447
  48.5 7.6 %collective-permute-start = (f32[392,128]{1,0:T(8,128)}, f32[392,128]{1,0:T(8,128)S(1)}, u32[]{:S(2)}, u32[]{:S(2)}) collective-permute-start(f32[392,128]{1,0:T(8,128)} %energy.1.bricks_ref), channel_id=1, source_target_pairs={{0,2},{1,3},{2,0},{3,1},{4,6},{5,7},{6,4},{7,5},{8,10},{9,11},{10,... | collective-permute-start | bytes 602120 | tf_op jit(solution)/shard_map/ppermute | solution.py:447
  54.1 2.7 %copy-start.3 = (f32[392,128]{1,0:T(8,128)}, f32[392,128]{1,0:T(8,128)S(1)}, u32[]{:S(2)}) copy-start(f32[392,128]{1,0:T(8,128)S(1)} %collective-permute-done.2.bricks_ref) | copy-start | bytes 602116
  56.1 4.2 %copy-start.1 = (f32[392,128]{1,0:T(8,128)}, f32[392,128]{1,0:T(8,128)S(1)}, u32[]{:S(2)}) copy-start(f32[392,128]{1,0:T(8,128)S(1)} %collective-permute-done.refs_1_) | copy-start | bytes 602116
  56.1 4.2 %collective-permute-start.1 = (f32[392,128]{1,0:T(8,128)S(1)}, f32[392,128]{1,0:T(8,128)S(1)}, u32[]{:S(2)}, u32[]{:S(2)}) collective-permute-start(f32[392,128]{1,0:T(8,128)S(1)} %collective-permute-done.refs_1_), channel_id=1, source_target_pairs={{0,1},{1,0},{2,3},{3,2},{4,5},{5,4},{6,7},{7,6},{8,9},{9,8},{10,11... | collective-permute-start | bytes 602120 | tf_op jit(solution)/shard_map/ppermute | solution.py:447
  60.3 0.7 copy-start.2
where the time goes:
time: 68.8 us; the launch traced here: 68.5 us
  Pallas kernels  48.7 us (71%)
  starting transfers between devices  8.82 us (13%)
  waiting for transfers between devices  7.05 us (10%)
  other arithmetic  2.53 us (4%)
  local copies, waits for them, and re-layouts  1.4 us (2%)
    pallas_call x1, Pallas kernels, make_pieces(): pl.pallas_call(functools.partial(pieces_kernel, steps, per_step, slots, p...  22.1 us
    pallas_call x1, Pallas kernels, make_energy(): pl.pallas_call(functools.partial(energy_kernel, slots), in_specs=[pl.Bloc...  9.2 us
    pallas_call x1, Pallas kernels, make_x(): pl.pallas_call(functools.partial(x_kernel, total, half_size), in_specs=[s...  7.52 us
    all_to_all x1, starting transfers between devices, local(): got = lax.all_to_all(send, 'wide', split_axis=0, concat_axis=0, tiled=True)  7.33 us
    pallas_call x2, Pallas kernels, make_y(): pl.pallas_call(functools.partial(y_kernel, total), in_specs=[pl.BlockSpec...  7.05 us
    all_to_all x1, waiting for transfers between devices, local(): got = lax.all_to_all(send, 'wide', split_axis=0, concat_axis=0, tiled=True)  5.6 us
    pallas_call x1, Pallas kernels, make_tables(): pl.pallas_call(tables_kernel, out_specs=[vmem] * 4, out_shape=[y_shape, y...  2.83 us
    convert_element_type x4, other arithmetic, ids_of(): return bricks[total * SUB:].reshape(-1)[:total].astype(i32)  2.32 us
  transfers between devices with their start and end apart: 4, of which 2 were waited for; matrix products, arithmetic and copies ran while one was open for 3% of the time, Pallas kernels for 14%

commit v1 on v0

v1 whole, which is shorter than its diff:
```python
import functools
import math

import jax
import jax.numpy as jnp
from jax import lax
from jax.experimental import pallas as pl
from jax.experimental.pallas import tpu as pltpu
from jax.sharding import PartitionSpec as P

NX = 1024
NY = 1024
GRP = 128
BY = 32
BX = 32
LANES = 128
PARTS = 4
SUB = 8

f32 = jnp.float32
bf16 = jnp.bfloat16
i32 = jnp.int32

energy_coef = -0.75 * (3.0 / math.pi) ** (1.0 / 3.0)

COS_FIT = (0.999999989, -0.499999891, 0.0416664892, -0.00138878036, 2.47698836e-05, -2.70790308e-07, 1.72450917e-09)
SIN_FIT = (0.999999999, -0.166666659, 0.00833332129, -0.000198405341, 2.753585e-06, -2.47288117e-08, 1.36130988e-10)
TURN_HI = 6.28125
TURN_LO = 2.0 * math.pi - TURN_HI


def horner(w, fit):
    total = jnp.full_like(w, fit[-1])
    for term in fit[-2::-1]:
        total = total * w + term
    return total


def cos_any(angle):
    turns = jnp.floor(angle * (0.5 / math.pi) + 0.5)
    r = (angle - turns * TURN_HI) - turns * TURN_LO
    return horner(r * r, COS_FIT)


def cos_sin_turn(step, length):
    r = (step - length // 2).astype(f32) * (2.0 * math.pi / length)
    w = r * r
    return -horner(w, COS_FIT), -(r * horner(w, SIN_FIT))


def split(value):
    high = value.astype(bf16)
    return high, (value - high.astype(f32)).astype(bf16)


def dot3(lhs_high, lhs_low, rhs_high, rhs_low):
    dot = functools.partial(jnp.dot, preferred_element_type=f32)
    return dot(lhs_high, rhs_high) + dot(lhs_low, rhs_high) + dot(lhs_high, rhs_low)


def coarse_fine(value):
    shift = 1.5 * 2.0**19
    coarse = (value + shift) - shift
    return coarse, value - coarse


def pieces_kernel(
    count, slots, planes, groups_ref, brick_ref, blocks_ref, freq_ref, phase_ref,
    send_ref, count_ref, stage_ref, sems, mixed0, mixed1, rows0, rows1,
):
    row_bricks = NX // BX
    col_bricks = NY // BY
    wide_size = send_ref.shape[0]
    narrow_size = lax.axis_size("narrow")
    narrow = lax.axis_index("narrow")
    column_bricks = row_bricks // narrow_size
    flip = 2 * narrow < narrow_size
    lane = lax.broadcasted_iota(i32, (SUB, LANES), 1)
    row = lax.broadcasted_iota(i32, (BY, GRP), 0)
    mixed, rows = (mixed0, mixed1), (rows0, rows1)

    def fetch(b):
        return pltpu.make_async_copy(blocks_ref.at[b], stage_ref.at[b], sems.at[b])

    for b in range(count):
        fetch(b).start()
    zero = jnp.zeros((slots * SUB, LANES), f32)
    none = jnp.full((SUB, LANES), -1.0, f32)
    for w in range(wide_size):
        send_ref[w, : slots * SUB, :] = zero
        send_ref[w, slots * SUB :, :] = none
        count_ref[w] = 0

    def factors(side, b):
        q = brick_ref[b]
        xb = q % row_bricks
        yb = (q // row_bricks) % col_bricks
        zb = q // (row_bricks * col_bricks)
        ys = (yb * BY + row).astype(f32)
        xs = (xb * BX + jnp.where(flip, BX - 1 - row, row)).astype(f32)
        at = pl.ds(pl.multiple_of(groups_ref[side, b] * GRP, GRP), GRP)
        freq = freq_ref[:, at]
        phase = phase_ref[:, at]
        along_x = cos_any(xs * freq[0:1] + phase[0:1])
        along_y = cos_any(ys * freq[1:2] + phase[1:2])
        along_z = cos_any(jnp.broadcast_to(zb.astype(f32) * freq[2:3] + phase[2:3], (SUB, GRP)))
        return along_x, along_y * along_z[0:1]

    pair = 2 * SUB

    def prepare(b, k):
        along_x, along_y = factors(0, b)
        xa, xb = coarse_fine(along_x)
        ya, yb = coarse_fine(along_y)
        rows_ref = rows[k]
        rows_ref[0] = xa
        rows_ref[1] = xb
        halves = []
        for h in range(BY // pair):
            at = slice(h * pair, (h + 1) * pair)
            halves.append((ya[at].astype(bf16), yb[at].astype(bf16), along_y[at].astype(bf16)))
        block = jnp.concatenate(split(stage_ref[b]), axis=1)
        block = jnp.concatenate([block, block], axis=0)
        per_part = BY * BX // pair // PARTS
        for part in range(PARTS):
            coarse, fine = [], []
            for tile in range(part * per_part, (part + 1) * per_part):
                x = tile % BX
                y_a, y_b, y_all = halves[tile // BX]
                x_a, x_b = (
                    jnp.concatenate([rows_ref[p, pl.ds(x, SUB, stride=0), :]] * 2, axis=0).astype(bf16)
                    for p in range(2)
                )
                coarse.append(x_a * y_a)
                fine.append(x_a * y_b + x_b * y_all)
            left = jnp.concatenate([jnp.concatenate(coarse, axis=0), jnp.concatenate(fine, axis=0)], axis=1)
            at = slice(part * per_part * pair, (part + 1) * per_part * pair)
            mixed[k][at, :] = jnp.dot(left, block, preferred_element_type=f32)
            yield

    def finish(b, k):
        along_x, along_y = factors(1, b)
        rows_ref = rows[k]
        rows_ref[2] = along_x
        tiles = [along_y[g * SUB : (g + 1) * SUB] for g in range(BY // SUB)]

        def row_sums(first, size):
            if size == 1:
                g, x = first // BX, first % BX
                at = slice((((g // 2) * BX + x) * 2 + g % 2) * SUB, (((g // 2) * BX + x) * 2 + g % 2 + 1) * SUB)
                value = mixed[k][at, :GRP] + mixed[k][at, GRP:]
                return value * (rows_ref[2, pl.ds(x, SUB, stride=0), :] * tiles[g])
            bit = size // 2
            one, two = row_sums(first, bit), row_sums(first + bit, bit)
            return merge(one, two, bit)

        def merge(one, two, bit):
            odd = (lane & bit) != 0
            return jnp.where(odd, two, one) + pltpu.roll(jnp.where(odd, one, two), bit, 1)

        sums = []
        for part in range(PARTS):
            sums.append(row_sums(part * (LANES // PARTS), LANES // PARTS))
            yield
        while len(sums) > 1:
            bit = LANES // len(sums)
            sums = [merge(one, two, bit) for one, two in zip(sums[::2], sums[1::2])]
        value = sums[0]
        q = brick_ref[b]
        zb = q // (row_bricks * col_bricks)
        home = zb // planes
        yb = (q // row_bricks) % col_bricks
        brick = ((zb % planes) * col_bricks + yb) * column_bricks + (q % row_bricks - narrow * column_bricks)
        rank = count_ref[home]
        count_ref[home] = rank + 1
        send_ref[home, pl.ds(pl.multiple_of(rank * SUB, SUB), SUB), :] = value
        send_ref[home, pl.ds(slots * SUB + rank, 1), :] = jnp.full((1, LANES), 1.0, f32) * brick.astype(f32)

    def weave(*works):
        works = list(works)
        while works:
            works = [work for work in works if next(work, works) is not works]

    fetch(0).wait()
    weave(prepare(0, 0))

    def two_blocks(i, carry):
        b = 2 * i
        fetch(b + 1).wait()
        fetch(b + 2).wait()
        weave(prepare(b + 1, 1), finish(b, 0))
        weave(prepare(b + 2, 0), finish(b + 1, 1))
        return carry

    lax.fori_loop(0, count // 2 - 1, two_blocks, 0)
    fetch(count - 1).wait()
    weave(prepare(count - 1, 1), finish(count - 2, 0))
    weave(finish(count - 1, 1))


def make_pieces(blocks, groups, bricks, freq, phase, wide_size, slots, planes):
    count = blocks.shape[0]
    assert count % 2 == 0 and count >= 2
    rows = slots * SUB + SUB
    vmem = pl.BlockSpec(memory_space=pltpu.VMEM)
    smem = pl.BlockSpec(memory_space=pltpu.SMEM)
    mixed = pltpu.VMEM((BY * BX, 2 * GRP), f32)
    return pl.pallas_call(
        functools.partial(pieces_kernel, count, slots, planes),
        in_specs=[smem, smem, pl.BlockSpec(memory_space=pl.ANY), vmem, vmem],
        out_specs=vmem,
        out_shape=jax.ShapeDtypeStruct((wide_size, rows, LANES), f32),
        scratch_shapes=[
            pltpu.SMEM((wide_size,), i32),
            pltpu.VMEM((count, GRP, GRP), f32),
            pltpu.SemaphoreType.DMA((count,)),
            mixed, mixed,
            pltpu.VMEM((3, BX, GRP), f32), pltpu.VMEM((3, BX, GRP), f32),
        ],
        name="pieces",
    )(groups.T, bricks, blocks, freq, phase)


def energy_kernel(slots, got_ref, core_ref, out_ref, ids_ref, first_ref, valence_ref, cells_ref, sem):
    wide_size = got_ref.shape[0]
    total = wide_size * slots
    narrow_size = lax.axis_size("narrow")
    narrow = lax.axis_index("narrow")
    column_bricks = core_ref.shape[1] // BX
    tiles = LANES // BX
    flip = 2 * narrow < narrow_size
    lane = lax.broadcasted_iota(i32, (SUB, LANES), 1)
    sub = lax.broadcasted_iota(i32, (SUB, LANES), 0)
    group = lane // BX

    fetch = pltpu.make_async_copy(got_ref.at[:, pl.ds(slots * SUB, SUB), :], ids_ref, sem)
    fetch.start()

    def piece(s):
        return got_ref[s // slots, (s % slots) * SUB : (s % slots + 1) * SUB, :]

    for s in range(total):
        valence_ref[s * SUB : (s + 1) * SUB, :] = jnp.zeros((SUB, LANES), f32)
    fetch.wait()
    bricks = [jnp.maximum(ids_ref[s // slots, s % slots, 0], 0.0).astype(i32) for s in range(total)]
    for s in range(total - 1, -1, -1):
        first_ref[bricks[s]] = s
    owners = [first_ref[bricks[s]] for s in range(total)]
    for s in range(total):
        rows = pl.ds(pl.multiple_of(owners[s] * SUB, SUB), SUB)
        valence_ref[rows, :] = valence_ref[rows, :] + piece(s)
    head = jnp.full((SUB, LANES), -1.0, f32)
    mirror = jnp.where(flip, lane - lane % BX + (BX - 1 - lane % BX), lane)
    for s in range(total):
        at = bricks[s]
        column = at % column_bricks
        placed = jnp.where(flip, at - column + (column_bricks - 1 - column), at)
        mark = jnp.where(owners[s] == s, placed, -1).astype(f32)
        head = jnp.where((lane == s % LANES) & (sub == s // LANES), mark, head)
        y0 = pl.multiple_of((at // column_bricks) * BY, BY)
        lanes = pl.ds(pl.multiple_of((column // tiles) * LANES, LANES), LANES)
        block = core_ref[pl.ds(y0, BY), lanes]
        first = column % tiles
        value = None
        for g in range(tiles):
            moved = pltpu.roll(block[g * SUB : (g + 1) * SUB], ((g - first + tiles) % tiles) * BX, 1)
            value = moved if value is None else jnp.where(group == g, moved, value)
        cells_ref[s * SUB : (s + 1) * SUB, :] = jnp.take_along_axis(value, mirror, axis=1)

    def four_thirds(value):
        size = jnp.maximum(jnp.abs(value), 1e-30)
        inverse = jnp.exp2(jnp.log2(size) * (-1.0 / 3.0))
        inverse = inverse * (4.0 - size * (inverse * inverse * inverse)) * (1.0 / 3.0)
        return size * (size * (inverse * inverse))

    core = cells_ref[...]
    rho = core + valence_ref[...]
    out_ref[: total * SUB, :] = energy_coef * (four_thirds(rho) - four_thirds(core))
    out_ref[total * SUB :, :] = head


def make_energy(got, core, slots):
    wide_size = got.shape[0]
    total = wide_size * slots
    bricks = (core.shape[0] // BY) * (core.shape[1] // BX)
    vmem = pl.BlockSpec(memory_space=pltpu.VMEM)
    return pl.pallas_call(
        functools.partial(energy_kernel, slots),
        in_specs=[vmem, vmem],
        out_specs=vmem,
        out_shape=jax.ShapeDtypeStruct(((total + 1) * SUB, LANES), f32),
        scratch_shapes=[
            pltpu.SMEM((wide_size, SUB, LANES), f32),
            pltpu.SMEM((bricks,), i32),
            pltpu.VMEM((total * SUB, LANES), f32),
            pltpu.VMEM((total * SUB, LANES), f32),
            pltpu.SemaphoreType.DMA,
        ],
        name="energy",
    )(got, core)


def tables_kernel(wy_high, wy_low, wx_high, wx_low):
    rows_all = NY // lax.axis_size("narrow")
    narrow = lax.axis_index("narrow")
    half = rows_all // 2
    depth = NY // 2
    lane = lax.broadcasted_iota(i32, (half, LANES), 1)
    row = lax.broadcasted_iota(i32, (half, LANES), 0)
    for p in range(2):
        wave = rows_all * narrow + 2 * row + p
        base_cos, base_sin = cos_sin_turn((wave * lane) % NY, NY)
        for t in range(depth // LANES):
            jump_cos, jump_sin = cos_sin_turn((wave[:SUB] * (t * LANES)) % NY, NY)
            jump_cos = jnp.concatenate([jump_cos] * (half // SUB), axis=0)
            jump_sin = jnp.concatenate([jump_sin] * (half // SUB), axis=0)
            at = slice(t * LANES, (t + 1) * LANES)
            for part, value in (
                (0, base_cos * jump_cos - base_sin * jump_sin),
                (1, -(base_sin * jump_cos + base_cos * jump_sin)),
            ):
                rows = slice(p * rows_all + part * half, p * rows_all + (part + 1) * half)
                wy_high[rows, at], wy_low[rows, at] = split(value)
    depth = NX // 2
    lane = lax.broadcasted_iota(i32, (depth, LANES), 1)
    place = 2 * lax.broadcasted_iota(i32, (depth, LANES), 0) + 1
    base_cos, base_sin = cos_sin_turn((place * lane) % (2 * NX), 2 * NX)
    for t in range(NX // 2 // LANES):
        jump_cos, jump_sin = cos_sin_turn((place[:SUB] * (t * LANES)) % (2 * NX), 2 * NX)
        jump_cos = jnp.concatenate([jump_cos] * (depth // SUB), axis=0)
        jump_sin = jnp.concatenate([jump_sin] * (depth // SUB), axis=0)
        at = slice(t * LANES, (t + 1) * LANES)
        for part, value in (
            (0, base_cos * jump_cos - base_sin * jump_sin),
            (1, base_sin * jump_cos + base_cos * jump_sin),
        ):
            rows = slice(part * depth, (part + 1) * depth)
            wx_high[rows, at], wx_low[rows, at] = split(value)


def make_tables(narrow_size):
    rows_all = NY // narrow_size
    y_shape = jax.ShapeDtypeStruct((2 * rows_all, NY // 2), bf16)
    x_shape = jax.ShapeDtypeStruct((NX, NX // 2), bf16)
    vmem = pl.BlockSpec(memory_space=pltpu.VMEM)
    return pl.pallas_call(
        tables_kernel,
        out_specs=[vmem] * 4,
        out_shape=[y_shape, y_shape, x_shape, x_shape],
        name="tables",
    )()


def along_y(total, bricks_ref, wy_high, wy_low, plane_ref, ids_ref, sem, out_ref):
    columns = plane_ref.shape[1]
    column_bricks = columns // BX
    tiles = LANES // BX
    lane = lax.broadcasted_iota(i32, (SUB, LANES), 1)
    group = lane // BX
    fetch = pltpu.make_async_copy(bricks_ref.at[pl.ds(total * SUB, SUB), :], ids_ref, sem)
    fetch.start()
    plane_ref[...] = jnp.zeros(plane_ref.shape, f32)
    fetch.wait()
    for s in range(total):
        brick = ids_ref[s // LANES, s % LANES].astype(i32)
        valid = brick >= 0
        at = jnp.maximum(brick, 0)
        column = at % column_bricks
        y0 = jnp.where(valid, (at // column_bricks) * BY, NY)
        lanes = pl.ds(pl.multiple_of((column // tiles) * LANES, LANES), LANES)
        value = pltpu.roll(bricks_ref[s * SUB : (s + 1) * SUB, :], (column % tiles) * BX, 1)
        mask = group == column % tiles
        for g in range(tiles):
            moved = value if g == 0 else pltpu.roll(value, LANES - g * BX, 1)
            rows = pl.ds(pl.multiple_of(y0 + g * SUB, SUB), SUB)
            pltpu.store(plane_ref.at[rows, lanes], moved, mask=mask)
    half = NY // 2
    rows_all = wy_high.shape[0] // 2
    upper = plane_ref[:half, :]
    lower = plane_ref[half:NY, :]
    for p in range(2):
        high, low = split(upper + lower if p == 0 else upper - lower)
        rows = slice(p * rows_all, (p + 1) * rows_all)
        value = dot3(wy_high[rows, :], wy_low[rows, :], high, low)
        for part in range(2):
            for t in range(columns // LANES):
                piece = value[part * rows_all // 2 : (part + 1) * rows_all // 2, t * LANES : (t + 1) * LANES]
                out_ref[part, t, pl.ds(p, rows_all // 2, stride=2), :] = piece


def y_kernel(total, bricks_ref, wy_high, wy_low, out_ref, plane_ref, ids_ref, sem):
    along_y(total, bricks_ref, wy_high, wy_low, plane_ref, ids_ref, sem, out_ref)


def make_y(bricks, tables, columns):
    total = bricks.shape[0] // SUB - 1
    vmem = pl.BlockSpec(memory_space=pltpu.VMEM)
    return pl.pallas_call(
        functools.partial(y_kernel, total),
        in_specs=[vmem, vmem, vmem],
        out_specs=vmem,
        out_shape=jax.ShapeDtypeStruct((2, columns // LANES, tables[0].shape[0] // 2, LANES), f32),
        scratch_shapes=[pltpu.VMEM((NY + BY, columns), f32), pltpu.SMEM((SUB, LANES), f32), pltpu.SemaphoreType.DMA],
        cost_estimate=pl.CostEstimate(flops=2 * 10**9, bytes_accessed=2 * 10**6, transcendentals=0),
        name="along_y",
    )(bricks, tables[0], tables[1])


def x_kernel(total, half_size, *refs):
    late_refs, refs = refs[:half_size], refs[half_size:]
    wy_high, wy_low, wx_high, wx_low = refs[:4]
    early_refs, out_ref, plane_ref = refs[4 : 4 + half_size], refs[4 + half_size], refs[5 + half_size]
    ids_ref, sem = refs[6 + half_size : 8 + half_size]
    late_y_refs = refs[8 + half_size :]
    narrow_size = 2 * half_size
    narrow = lax.axis_index("narrow")
    tiles = early_refs[0].shape[1]
    columns = tiles * LANES
    for k in range(half_size):
        along_y(total, late_refs[k], wy_high, wy_low, plane_ref, ids_ref, sem, late_y_refs[k])

    def whole(ref, part):
        return jnp.concatenate([ref[part, t] for t in range(tiles)], axis=1)

    u = v = None
    for mask in range(half_size):
        near_ref = early_refs[mask]
        far_ref = late_y_refs[half_size - 1 - mask]
        source = lax.bitwise_xor(narrow, mask)
        mirror = narrow_size - 1 - source
        sign = jnp.where(source < mirror, 1.0, -1.0).astype(f32)
        start = pl.multiple_of((jnp.maximum(source, mirror) - half_size) * columns, columns)
        cos_rows = pl.ds(start, columns)
        sin_rows = pl.ds(pl.multiple_of(NX // 2 + start, columns), columns)
        c = (wx_high[cos_rows, :], wx_low[cos_rows, :])
        s = (wx_high[sin_rows, :], wx_low[sin_rows, :])
        near = [whole(near_ref, part) for part in range(2)]
        far = [whole(far_ref, part) for part in range(2)]
        even = [split(a + b) for a, b in zip(near, far)]
        odd = [split((b - a) * sign) for a, b in zip(near, far)]
        u_new = dot3(*even[0], *c) + dot3(*odd[1], *s)
        v_new = dot3(*even[1], *c) - dot3(*odd[0], *s)
        u = u_new if u is None else u + u_new
        v = v_new if v is None else v + v_new
    lane = lax.broadcasted_iota(i32, (SUB, NX // 2), 1)
    phase_cos, phase_sin = cos_sin_turn((lane * (NX - 1)) % (2 * NX), 2 * NX)
    scale = 1.0 / math.sqrt(NX * NY)
    phase_cos, phase_sin = phase_cos[0:1] * scale, phase_sin[0:1] * scale
    out_ref[0] = u * phase_cos + v * phase_sin
    out_ref[1] = v * phase_cos - u * phase_sin


def make_x(late, tables, early):
    half_size = len(early)
    total = late[0].shape[0] // SUB - 1
    rows_all = tables[0].shape[0] // 2
    columns = early[0].shape[1] * LANES
    vmem = pl.BlockSpec(memory_space=pltpu.VMEM)
    return pl.pallas_call(
        functools.partial(x_kernel, total, half_size),
        in_specs=[vmem] * (4 + 2 * half_size),
        out_specs=vmem,
        out_shape=jax.ShapeDtypeStruct((2, rows_all, NX // 2), f32),
        scratch_shapes=[pltpu.VMEM((NY + BY, columns), f32), pltpu.SMEM((SUB, LANES), f32), pltpu.SemaphoreType.DMA]
        + [pltpu.VMEM(early[0].shape, f32)] * half_size,
        name="along_x",
    )(*late, *tables, *early)


def local(density_blocks, block_groups, block_brick, orbital_freq, orbital_phase, core_density):
    wide_size = lax.axis_size("wide")
    narrow_size = lax.axis_size("narrow")
    block_count = density_blocks.shape[0]
    slots = (2 * block_count + wide_size - 1) // wide_size
    planes, grid_rows, columns = core_density.shape
    half_size = narrow_size // 2
    assert narrow_size & (narrow_size - 1) == 0 and planes == 1 and slots <= SUB
    send = make_pieces(
        density_blocks, block_groups, block_brick, orbital_freq, orbital_phase, wide_size, slots, planes
    )
    got = lax.all_to_all(send, "wide", split_axis=0, concat_axis=0, tiled=True)
    own = make_energy(got, core_density.reshape(grid_rows, columns), slots)

    def across(value, mask):
        return lax.ppermute(value, "narrow", [(i, i ^ mask) for i in range(narrow_size)])

    bricks = {0: own}
    step = half_size
    while step:
        bricks |= {mask | step: across(value, step) for mask, value in bricks.items()}
        step //= 2
    tables = make_tables(narrow_size)
    early = [make_y(bricks[mask], tables, columns) for mask in range(half_size)]
    late = [bricks[mask] for mask in range(half_size, narrow_size)]
    return make_x(late, tables, early)[None]


def solution(mesh):
    return jax.shard_map(
        local,
        mesh=mesh,
        in_specs=(
            P(("wide", "narrow"), None, None),
            P(("wide", "narrow"), None),
            P(("wide", "narrow")),
            P(),
            P(),
            P("wide", None, "narrow"),
        ),
        out_specs=P("wide", None, "narrow", None),
        check_vma=False,
    )
```

time: 68.8 us -> 61 us (0.89)
  blocking collectives: 0 us -> 15.9 us
  Pallas kernels: 48.7 us -> 40.2 us
  starting transfers between devices: 8.82 us -> 1.55 us
  waiting for transfers between devices: 7.05 us -> 1.61 us
  other arithmetic: 2.53 us -> 0 us
    all_to_all x0 -> x1, blocking collectives: none -> 15.9 us  [local(): got = lax.all_to_all(send, 'wide', split_axis=0, concat_axis=0, tiled=True)]
    pallas_call x5, Pallas kernels: 45.8 us -> 37.4 us  [the longest x1 14.5 us: make_pieces(): pl.pallas_call(functools.partial(pieces_kernel, count, slots, planes), in...]
    all_to_all x1 -> x0, starting transfers between devices: 7.33 us -> none  [local(): got = lax.all_to_all(send, 'wide', split_axis=0, concat_axis=0, tiled=True)]
    all_to_all x1 -> x0, waiting for transfers between devices: 5.6 us -> none  [local(): got = lax.all_to_all(send, 'wide', split_axis=0, concat_axis=0, tiled=True)]
    convert_element_type x5 -> x0, other arithmetic: 2.53 us -> none  [the longest x4 2.32 us: ids_of(): return bricks[total * SUB:].reshape(-1)[:total].astype(i32)]
    unnamed x8 -> x6, local copies, waits for them, and re-layouts: 0.12 us -> 1.35 us
  transfers between devices with their start and end apart: 4 -> 3, of which waited for: 2 -> 1; matrix products, arithmetic and copies ran while one was open for 3% -> 0% of each run, Pallas kernels for 14% -> 19%
where the time goes in v1:
time: 61 us; the launch traced here: 60.7 us
  Pallas kernels  40.2 us (66%)
  blocking collectives  15.9 us (26%)
  waiting for transfers between devices  1.61 us (3%)
  starting transfers between devices  1.55 us (3%)
  local copies, waits for them, and re-layouts  1.35 us (2%)
    all_to_all x1, blocking collectives, local(): got = lax.all_to_all(send, 'wide', split_axis=0, concat_axis=0, tiled=True)  15.9 us
    pallas_call x1, Pallas kernels, make_pieces(): pl.pallas_call(functools.partial(pieces_kernel, count, slots, planes), in...  14.5 us
    pallas_call x1, Pallas kernels, make_x(): pl.pallas_call(functools.partial(x_kernel, total, half_size), in_specs=[v...  8.96 us
    pallas_call x2, Pallas kernels, make_y(): pl.pallas_call(functools.partial(y_kernel, total), in_specs=[vmem, vmem,...  8.55 us
    pallas_call x1, Pallas kernels, make_energy(): pl.pallas_call(functools.partial(energy_kernel, slots), in_specs=[vmem, v...  5.35 us
    pallas_call x1, Pallas kernels, make_tables(): pl.pallas_call(tables_kernel, out_specs=[vmem] * 4, out_shape=[y_shape, y...  2.84 us
    ppermute x3, waiting for transfers between devices, across(): lax.ppermute(value, 'narrow', [(i, i ^ mask) for i in range(narrow_size)])  1.61 us
    ppermute x3, starting transfers between devices, across(): lax.ppermute(value, 'narrow', [(i, i ^ mask) for i in range(narrow_size)])  1.55 us
  transfers between devices with their start and end apart: 3, of which 1 were waited for; matrix products, arithmetic and copies ran while one was open for 0% of the time, Pallas kernels for 19%

profile of v1, /device:TPU:0, one launch (start us, length us, event | category | flops | bytes accessed | tf_op | source)
XLA Modules:
  0.0 60.7 jit_solution(539482467201077492)
XLA Ops:
  0.0 14.5 %pieces.1 = f32[8,56,128]{2,1,0:T(8,128)} custom-call(s32[2,24]{1,0:T(2,128)} %bitcast.4, s32[24]{0:T(128)} %brick_ref.1, f32[24,128,128]{2,1,0:T(8,128)} %blocks_ref.1, f32[3,8192]{1,0:T(4,128)} %freq_ref.1, f32[3,8192]{1,0:T(4,128)} %phase_ref.1), custom_call_target="tpu_custom_call" | custom-call | tf_op jit(solution)/shard_map/pieces/pallas_call | solution.py:208
  14.5 15.9 %all_to_all.5.got_ref = f32[8,56,128]{2,1,0:T(8,128)} all-to-all(f32[8,56,128]{2,1,0:T(8,128)} %pieces.1), channel_id=1, replica_groups=mesh['wide'=8,'narrow'=4] {'wide'}, dimensions={0} | all-to-all | bytes 458752 | tf_op jit(solution)/shard_map/all_to_all | solution.py:481
  30.4 5.4 %energy.1.bricks_ref = f32[392,128]{1,0:T(8,128)} custom-call(f32[8,56,128]{2,1,0:T(8,128)} %all_to_all.5.got_ref, f32[1024,256]{1,0:T(8,128)} %bitcast.3), custom_call_target="tpu_custom_call" | custom-call | tf_op jit(solution)/shard_map/energy/pallas_call | solution.py:287
  35.8 1.5 %collective-permute-start = (f32[392,128]{1,0:T(8,128)}, f32[392,128]{1,0:T(8,128)S(1)}, u32[]{:S(2)}, u32[]{:S(2)}) collective-permute-start(f32[392,128]{1,0:T(8,128)} %energy.1.bricks_ref), channel_id=1, source_target_pairs={{0,2},{1,3},{2,0},{3,1},{4,6},{5,7},{6,4},{7,5},{8,10},{9,11},{10,... | collective-permute-start | bytes 602120 | tf_op jit(solution)/shard_map/ppermute | solution.py:485
  37.3 0.0 collective-permute-start.2
  37.3 2.8 %tables.1 = (bf16[512,512]{1,0:T(8,128)(2,1)}, bf16[512,512]{1,0:T(8,128)(2,1)}, bf16[1024,512]{1,0:T(8,128)(2,1)}, bf16[1024,512]{1,0:T(8,128)(2,1)}) custom-call(), custom_call_target="tpu_custom_call" | custom-call | tf_op jit(solution)/shard_map/tables/pallas_call | solution.py:346
  40.1 1.6 %collective-permute-done.refs_0_ = f32[392,128]{1,0:T(8,128)S(1)} collective-permute-done((f32[392,128]{1,0:T(8,128)}, f32[392,128]{1,0:T(8,128)S(1)}, u32[]{:S(2)}, u32[]{:S(2)}) %collective-permute-start) | collective-permute-done | bytes 200736 | tf_op jit(solution)/shard_map/ppermute | solution.py:485
  41.7 0.0 copy-start
  41.7 0.0 collective-permute-start.1
  41.8 4.3 %along_y.2.refs_6_ = f32[2,2,256,128]{3,2,1,0:T(8,128)} custom-call(f32[392,128]{1,0:T(8,128)} %energy.1.bricks_ref, bf16[512,512]{1,0:T(8,128)(2,1)} %get-tuple-element.9.wy_high.refs_2_, bf16[512,512]{1,0:T(8,128)(2,1)} %get-tuple-element.10.wy_low.refs_3_), custom_call_target="tpu_custom_call" | custom-call | flops 2000000000 | bytes 2000000 | tf_op jit(solution)/shard_map/along_y/pallas_call | solution.py:398
  46.1 0.0 copy-done
  46.1 0.0 collective-permute-done.2.bricks_ref
  46.1 0.0 copy-start.2
  46.1 0.7 %copy-done.2 = f32[392,128]{1,0:T(8,128)} copy-done((f32[392,128]{1,0:T(8,128)}, f32[392,128]{1,0:T(8,128)S(1)}, u32[]{:S(2)}) %copy-start.2) | copy-done | bytes 200728
  46.8 4.2 %along_y.3.refs_7_ = f32[2,2,256,128]{3,2,1,0:T(8,128)} custom-call(f32[392,128]{1,0:T(8,128)} %copy-done.2, bf16[512,512]{1,0:T(8,128)(2,1)} %get-tuple-element.9.wy_high.refs_2_, bf16[512,512]{1,0:T(8,128)(2,1)} %get-tuple-element.10.wy_low.refs_3_), custom_call_target="tpu_custom_call" | custom-call | flops 2000000000 | bytes 2000000 | tf_op jit(solution)/shard_map/along_y/pallas_call | solution.py:398
  51.0 0.0 collective-permute-done.1.refs_1_
  51.0 0.0 copy-start.1
  51.0 0.7 %copy-done.1 = f32[392,128]{1,0:T(8,128)} copy-done((f32[392,128]{1,0:T(8,128)}, f32[392,128]{1,0:T(8,128)S(1)}, u32[]{:S(2)}) %copy-start.1) | copy-done | bytes 200728
  51.7 9.0 %along_x.1 = f32[2,256,512]{2,1,0:T(8,128)} custom-call(f32[392,128]{1,0:T(8,128)} %copy-done, f32[392,128]{1,0:T(8,128)} %copy-done.1, bf16[512,512]{1,0:T(8,128)(2,1)} %get-tuple-element.9.wy_high.refs_2_, bf16[512,512]{1,0:T(8,128)(2,1)} %get-tuple-element.10.wy_low.refs_3_, bf16[1024,512]{1,0:T(8,128)(2,1)} %get-tuple-element.11.refs_4_, ...), custom_call_target="tpu_custom_call" | custom-call | tf_op jit(solution)/shard_map/along_x/pallas_call | solution.py:459
Async XLA Ops:
  35.8 6.0 %collective-permute-start = (f32[392,128]{1,0:T(8,128)}, f32[392,128]{1,0:T(8,128)S(1)}, u32[]{:S(2)}, u32[]{:S(2)}) collective-permute-start(f32[392,128]{1,0:T(8,128)} %energy.1.bricks_ref), channel_id=1, source_target_pairs={{0,2},{1,3},{2,0},{3,1},{4,6},{5,7},{6,4},{7,5},{8,10},{9,11},{10,... | collective-permute-start | bytes 602120 | tf_op jit(solution)/shard_map/ppermute | solution.py:485
  37.3 8.8 %collective-permute-start.2 = (f32[392,128]{1,0:T(8,128)}, f32[392,128]{1,0:T(8,128)S(1)}, u32[]{:S(2)}, u32[]{:S(2)}) collective-permute-start(f32[392,128]{1,0:T(8,128)} %energy.1.bricks_ref), channel_id=1, source_target_pairs={{0,1},{1,0},{2,3},{3,2},{4,5},{5,4},{6,7},{7,6},{8,9},{9,8},{10,11... | collective-permute-start | bytes 602120 | tf_op jit(solution)/shard_map/ppermute | solution.py:485
  41.7 4.3 %copy-start = (f32[392,128]{1,0:T(8,128)}, f32[392,128]{1,0:T(8,128)S(1)}, u32[]{:S(2)}) copy-start(f32[392,128]{1,0:T(8,128)S(1)} %collective-permute-done.refs_0_) | copy-start | bytes 602116
  41.7 9.3 %collective-permute-start.1 = (f32[392,128]{1,0:T(8,128)S(1)}, f32[392,128]{1,0:T(8,128)S(1)}, u32[]{:S(2)}, u32[]{:S(2)}) collective-permute-start(f32[392,128]{1,0:T(8,128)S(1)} %collective-permute-done.refs_0_), channel_id=1, source_target_pairs={{0,1},{1,0},{2,3},{3,2},{4,5},{5,4},{6,7},{7,6},{8,9},{9,8},{10,11... | collective-permute-start | bytes 602120 | tf_op jit(solution)/shard_map/ppermute | solution.py:485
  46.1 0.7 %copy-start.2 = (f32[392,128]{1,0:T(8,128)}, f32[392,128]{1,0:T(8,128)S(1)}, u32[]{:S(2)}) copy-start(f32[392,128]{1,0:T(8,128)S(1)} %collective-permute-done.2.bricks_ref) | copy-start | bytes 602116
  51.0 0.7 %copy-start.1 = (f32[392,128]{1,0:T(8,128)}, f32[392,128]{1,0:T(8,128)S(1)}, u32[]{:S(2)}) copy-start(f32[392,128]{1,0:T(8,128)S(1)} %collective-permute-done.1.refs_1_) | copy-start | bytes 602116

commit v2 on v1

--- a/solution.py
+++ b/solution.py
@@ -15,6 +15,7 @@
 BX = 32
 LANES = 128
 PARTS = 4
+VMEM_LIMIT = 16 * 2**20
 SUB = 8
 
 f32 = jnp.float32
@@ -46,6 +47,14 @@
     r = (step - length // 2).astype(f32) * (2.0 * math.pi / length)
     w = r * r
     return -horner(w, COS_FIT), -(r * horner(w, SIN_FIT))
+
+
+def on_chip(value):
+    return pltpu.with_memory_space_constraint(value, pltpu.VMEM)
+
+
+def off_chip(value):
+    return pltpu.with_memory_space_constraint(value, pltpu.HBM)
 
 
 def split(value):
@@ -174,7 +183,8 @@
         rank = count_ref[home]
         count_ref[home] = rank + 1
         send_ref[home, pl.ds(pl.multiple_of(rank * SUB, SUB), SUB), :] = value
-        send_ref[home, pl.ds(slots * SUB + rank, 1), :] = jnp.full((1, LANES), 1.0, f32) * brick.astype(f32)
+        head = send_ref[home, slots * SUB :, :]
+        send_ref[home, slots * SUB :, :] = jnp.where(lane == rank, brick.astype(f32), head)
 
     def weave(*works):
         works = list(works)
@@ -209,7 +219,7 @@
         functools.partial(pieces_kernel, count, slots, planes),
         in_specs=[smem, smem, pl.BlockSpec(memory_space=pl.ANY), vmem, vmem],
         out_specs=vmem,
-        out_shape=jax.ShapeDtypeStruct((wide_size, rows, LANES), f32),
+        out_shape=pltpu.VMEM((wide_size, rows, LANES), f32),
         scratch_shapes=[
             pltpu.SMEM((wide_size,), i32),
             pltpu.VMEM((count, GRP, GRP), f32),
@@ -217,23 +227,35 @@
             mixed, mixed,
             pltpu.VMEM((3, BX, GRP), f32), pltpu.VMEM((3, BX, GRP), f32),
         ],
+        compiler_params=pltpu.CompilerParams(vmem_limit_bytes=VMEM_LIMIT),
         name="pieces",
-    )(groups.T, bricks, blocks, freq, phase)
-
-
-def energy_kernel(slots, got_ref, core_ref, out_ref, ids_ref, first_ref, valence_ref, cells_ref, sem):
+    )(*map(off_chip, (groups.T, bricks, blocks, freq, phase)))
+
+
+def bits_of(count):
+    assert count & (count - 1) == 0
+    return count.bit_length() - 1
+
+
+def energy_kernel(slots, got_ref, core_ref, out_ref, codes_ref, code_ref, first_ref, valence_ref, cells_ref, sem):
     wide_size = got_ref.shape[0]
     total = wide_size * slots
     narrow_size = lax.axis_size("narrow")
     narrow = lax.axis_index("narrow")
     column_bricks = core_ref.shape[1] // BX
+    column_bits = bits_of(column_bricks)
     tiles = LANES // BX
     flip = 2 * narrow < narrow_size
     lane = lax.broadcasted_iota(i32, (SUB, LANES), 1)
     sub = lax.broadcasted_iota(i32, (SUB, LANES), 0)
     group = lane // BX
 
-    fetch = pltpu.make_async_copy(got_ref.at[:, pl.ds(slots * SUB, SUB), :], ids_ref, sem)
+    heads = []
+    for w in range(0, wide_size, SUB):
+        head = jnp.concatenate([got_ref[w + k, slots * SUB : slots * SUB + 1, :] for k in range(SUB)], axis=0)
+        heads.append(head)
+        codes_ref[w : w + SUB, :] = jnp.maximum(head, 0.0).astype(i32)
+    fetch = pltpu.make_async_copy(codes_ref, code_ref, sem)
     fetch.start()
 
     def piece(s):
@@ -241,29 +263,26 @@
 
     for s in range(total):
         valence_ref[s * SUB : (s + 1) * SUB, :] = jnp.zeros((SUB, LANES), f32)
+    mirror = jnp.where(flip, lane - lane % BX + (BX - 1 - lane % BX), lane)
     fetch.wait()
-    bricks = [jnp.maximum(ids_ref[s // slots, s % slots, 0], 0.0).astype(i32) for s in range(total)]
+    bricks = [code_ref[s // slots, s % slots] for s in range(total)]
     for s in range(total - 1, -1, -1):
         first_ref[bricks[s]] = s
-    owners = [first_ref[bricks[s]] for s in range(total)]
     for s in range(total):
-        rows = pl.ds(pl.multiple_of(owners[s] * SUB, SUB), SUB)
+        owner = first_ref[bricks[s]]
+        rows = pl.ds(pl.multiple_of(owner * SUB, SUB), SUB)
         valence_ref[rows, :] = valence_ref[rows, :] + piece(s)
-    head = jnp.full((SUB, LANES), -1.0, f32)
-    mirror = jnp.where(flip, lane - lane % BX + (BX - 1 - lane % BX), lane)
-    for s in range(total):
-        at = bricks[s]
-        column = at % column_bricks
-        placed = jnp.where(flip, at - column + (column_bricks - 1 - column), at)
-        mark = jnp.where(owners[s] == s, placed, -1).astype(f32)
-        head = jnp.where((lane == s % LANES) & (sub == s // LANES), mark, head)
-        y0 = pl.multiple_of((at // column_bricks) * BY, BY)
-        lanes = pl.ds(pl.multiple_of((column // tiles) * LANES, LANES), LANES)
-        block = core_ref[pl.ds(y0, BY), lanes]
-        first = column % tiles
+        mark = jnp.where(owner == s, bricks[s], -1).astype(f32)
+        w = s // slots
+        heads[w // SUB] = jnp.where((lane == s % slots) & (sub == w % SUB), mark, heads[w // SUB])
+        column = bricks[s] & (column_bricks - 1)
+        y0 = pl.multiple_of((bricks[s] >> column_bits) * BY, BY)
+        lanes = pl.ds(pl.multiple_of((column >> bits_of(tiles)) * LANES, LANES), LANES)
+        first = column & (tiles - 1)
         value = None
         for g in range(tiles):
-            moved = pltpu.roll(block[g * SUB : (g + 1) * SUB], ((g - first + tiles) % tiles) * BX, 1)
+            block = core_ref[pl.ds(y0 + g * SUB, SUB), lanes]
+            moved = pltpu.roll(block, ((g - first) & (tiles - 1)) * BX, 1)
             value = moved if value is None else jnp.where(group == g, moved, value)
         cells_ref[s * SUB : (s + 1) * SUB, :] = jnp.take_along_axis(value, mirror, axis=1)
 
@@ -276,7 +295,12 @@
     core = cells_ref[...]
     rho = core + valence_ref[...]
     out_ref[: total * SUB, :] = energy_coef * (four_thirds(rho) - four_thirds(core))
-    out_ref[total * SUB :, :] = head
+    for k, head in enumerate(heads):
+        code = jnp.maximum(head, 0.0).astype(i32)
+        column = code & (column_bricks - 1)
+        placed = jnp.where(flip, code - column + (column_bricks - 1 - column), code)
+        rows = slice(total * SUB + k * SUB, total * SUB + (k + 1) * SUB)
+        out_ref[rows, :] = jnp.where(head < 0.0, -1.0, placed.astype(f32))
 
 
 def make_energy(got, core, slots):
@@ -288,16 +312,18 @@
         functools.partial(energy_kernel, slots),
         in_specs=[vmem, vmem],
         out_specs=vmem,
-        out_shape=jax.ShapeDtypeStruct(((total + 1) * SUB, LANES), f32),
+        out_shape=pltpu.VMEM((total * SUB + wide_size, LANES), f32),
         scratch_shapes=[
-            pltpu.SMEM((wide_size, SUB, LANES), f32),
+            pltpu.VMEM((wide_size, LANES), i32),
+            pltpu.SMEM((wide_size, LANES), i32),
             pltpu.SMEM((bricks,), i32),
             pltpu.VMEM((total * SUB, LANES), f32),
             pltpu.VMEM((total * SUB, LANES), f32),
             pltpu.SemaphoreType.DMA,
         ],
+        compiler_params=pltpu.CompilerParams(vmem_limit_bytes=VMEM_LIMIT),
         name="energy",
-    )(got, core)
+    )(on_chip(got), core)
 
 
 def tables_kernel(wy_high, wy_low, wx_high, wx_low):
@@ -340,131 +366,155 @@
 
 def make_tables(narrow_size):
     rows_all = NY // narrow_size
-    y_shape = jax.ShapeDtypeStruct((2 * rows_all, NY // 2), bf16)
-    x_shape = jax.ShapeDtypeStruct((NX, NX // 2), bf16)
+    y_shape = pltpu.VMEM((2 * rows_all, NY // 2), bf16)
+    x_shape = pltpu.VMEM((NX, NX // 2), bf16)
     vmem = pl.BlockSpec(memory_space=pltpu.VMEM)
     return pl.pallas_call(
         tables_kernel,
         out_specs=[vmem] * 4,
         out_shape=[y_shape, y_shape, x_shape, x_shape],
+        compiler_params=pltpu.CompilerParams(vmem_limit_bytes=VMEM_LIMIT),
         name="tables",
     )()
 
 
-def along_y(total, bricks_ref, wy_high, wy_low, plane_ref, ids_ref, sem, out_ref):
-    columns = plane_ref.shape[1]
-    column_bricks = columns // BX
+def along_y(slots, columns, bricks_ref, wy_high, wy_low, scratch, out_ref):
+    plane_ref, codes_ref, code_ref, sem = scratch
+    wide_size = codes_ref.shape[0]
+    total = wide_size * slots
+    column_bits = bits_of(columns // BX)
     tiles = LANES // BX
-    lane = lax.broadcasted_iota(i32, (SUB, LANES), 1)
-    group = lane // BX
-    fetch = pltpu.make_async_copy(bricks_ref.at[pl.ds(total * SUB, SUB), :], ids_ref, sem)
+    blocks = columns // LANES
+    depth = NY + BY
+    group = lax.broadcasted_iota(i32, (SUB, LANES), 1) // BX
+    head = bricks_ref[total * SUB :, :]
+    brick = jnp.maximum(head, 0.0).astype(i32)
+    column = brick & (columns // BX - 1)
+    row = (column >> bits_of(tiles)) * depth + jnp.where(head < 0.0, NY, (brick >> column_bits) * BY)
+    codes_ref[...] = row * tiles + (column & (tiles - 1))
+    fetch = pltpu.make_async_copy(codes_ref, code_ref, sem)
     fetch.start()
     plane_ref[...] = jnp.zeros(plane_ref.shape, f32)
     fetch.wait()
     for s in range(total):
-        brick = ids_ref[s // LANES, s % LANES].astype(i32)
-        valid = brick >= 0
-        at = jnp.maximum(brick, 0)
-        column = at % column_bricks
-        y0 = jnp.where(valid, (at // column_bricks) * BY, NY)
-        lanes = pl.ds(pl.multiple_of((column // tiles) * LANES, LANES), LANES)
-        value = pltpu.roll(bricks_ref[s * SUB : (s + 1) * SUB, :], (column % tiles) * BX, 1)
-        mask = group == column % tiles
+        code = code_ref[s // slots, s % slots]
+        first = code & (tiles - 1)
+        row = code >> bits_of(tiles)
+        value = pltpu.roll(bricks_ref[s * SUB : (s + 1) * SUB, :], first * BX, 1)
+        mask = group == first
         for g in range(tiles):
             moved = value if g == 0 else pltpu.roll(value, LANES - g * BX, 1)
-            rows = pl.ds(pl.multiple_of(y0 + g * SUB, SUB), SUB)
-            pltpu.store(plane_ref.at[rows, lanes], moved, mask=mask)
+            rows = pl.ds(pl.multiple_of(row + g * SUB, SUB), SUB)
+            pltpu.store(plane_ref.at[rows, :], moved, mask=mask)
     half = NY // 2
     rows_all = wy_high.shape[0] // 2
-    upper = plane_ref[:half, :]
-    lower = plane_ref[half:NY, :]
+    upper = jnp.concatenate([plane_ref[t * depth : t * depth + half, :] for t in range(blocks)], axis=1)
+    lower = jnp.concatenate([plane_ref[t * depth + half : t * depth + NY, :] for t in range(blocks)], axis=1)
+    dot = functools.partial(jnp.dot, preferred_element_type=f32)
     for p in range(2):
         high, low = split(upper + lower if p == 0 else upper - lower)
         rows = slice(p * rows_all, (p + 1) * rows_all)
-        value = dot3(wy_high[rows, :], wy_low[rows, :], high, low)
+        table = wy_high[rows, :]
+        value = dot(jnp.concatenate([table, wy_low[rows, :]], axis=0), high)
+        value = value[:rows_all] + value[rows_all:] + dot(table, low)
         for part in range(2):
-            for t in range(columns // LANES):
+            for t in range(blocks):
                 piece = value[part * rows_all // 2 : (part + 1) * rows_all // 2, t * LANES : (t + 1) * LANES]
                 out_ref[part, t, pl.ds(p, rows_all // 2, stride=2), :] = piece
 
 
-def y_kernel(total, bricks_ref, wy_high, wy_low, out_ref, plane_ref, ids_ref, sem):
-    along_y(total, bricks_ref, wy_high, wy_low, plane_ref, ids_ref, sem, out_ref)
-
-
-def make_y(bricks, tables, columns):
-    total = bricks.shape[0] // SUB - 1
+def along_y_scratch(wide_size, columns):
+    return [
+        pltpu.VMEM((columns // LANES * (NY + BY), LANES), f32),
+        pltpu.VMEM((wide_size, LANES), i32),
+        pltpu.SMEM((wide_size, LANES), i32),
+        pltpu.SemaphoreType.DMA,
+    ]
+
+
+def y_kernel(slots, columns, bricks_ref, wy_high, wy_low, out_ref, *scratch):
+    along_y(slots, columns, bricks_ref, wy_high, wy_low, scratch, out_ref)
+
+
+def make_y(bricks, tables, columns, wide_size, slots):
     vmem = pl.BlockSpec(memory_space=pltpu.VMEM)
     return pl.pallas_call(
-        functools.partial(y_kernel, total),
+        functools.partial(y_kernel, slots, columns),
         in_specs=[vmem, vmem, vmem],
         out_specs=vmem,
-        out_shape=jax.ShapeDtypeStruct((2, columns // LANES, tables[0].shape[0] // 2, LANES), f32),
-        scratch_shapes=[pltpu.VMEM((NY + BY, columns), f32), pltpu.SMEM((SUB, LANES), f32), pltpu.SemaphoreType.DMA],
+        out_shape=pltpu.VMEM((2, columns // LANES, tables[0].shape[0] // 2, LANES), f32),
+        scratch_shapes=along_y_scratch(wide_size, columns),
         cost_estimate=pl.CostEstimate(flops=2 * 10**9, bytes_accessed=2 * 10**6, transcendentals=0),
+        compiler_params=pltpu.CompilerParams(vmem_limit_bytes=VMEM_LIMIT),
         name="along_y",
-    )(bricks, tables[0], tables[1])
-
-
-def x_kernel(total, half_size, *refs):
-    late_refs, refs = refs[:half_size], refs[half_size:]
-    wy_high, wy_low, wx_high, wx_low = refs[:4]
-    early_refs, out_ref, plane_ref = refs[4 : 4 + half_size], refs[4 + half_size], refs[5 + half_size]
-    ids_ref, sem = refs[6 + half_size : 8 + half_size]
-    late_y_refs = refs[8 + half_size :]
-    narrow_size = 2 * half_size
+    )(on_chip(bricks), on_chip(tables[0]), on_chip(tables[1]))
+
+
+def x_kernel(slots, columns, mask, first, last, *refs):
+    bricks_ref, near_ref, wy_high, wy_low, wx_high, wx_low = refs[:6]
+    sum_ref = None if first else refs[6]
+    out_ref, far_ref = refs[6 + (not first)], refs[7 + (not first)]
+    scratch = refs[8 + (not first) :]
+    half_size = lax.axis_size("narrow") // 2
     narrow = lax.axis_index("narrow")
-    tiles = early_refs[0].shape[1]
-    columns = tiles * LANES
-    for k in range(half_size):
-        along_y(total, late_refs[k], wy_high, wy_low, plane_ref, ids_ref, sem, late_y_refs[k])
+    blocks = columns // LANES
+    along_y(slots, columns, bricks_ref, wy_high, wy_low, scratch, far_ref)
 
     def whole(ref, part):
-        return jnp.concatenate([ref[part, t] for t in range(tiles)], axis=1)
-
-    u = v = None
-    for mask in range(half_size):
-        near_ref = early_refs[mask]
-        far_ref = late_y_refs[half_size - 1 - mask]
-        source = lax.bitwise_xor(narrow, mask)
-        mirror = narrow_size - 1 - source
-        sign = jnp.where(source < mirror, 1.0, -1.0).astype(f32)
-        start = pl.multiple_of((jnp.maximum(source, mirror) - half_size) * columns, columns)
-        cos_rows = pl.ds(start, columns)
-        sin_rows = pl.ds(pl.multiple_of(NX // 2 + start, columns), columns)
-        c = (wx_high[cos_rows, :], wx_low[cos_rows, :])
-        s = (wx_high[sin_rows, :], wx_low[sin_rows, :])
-        near = [whole(near_ref, part) for part in range(2)]
-        far = [whole(far_ref, part) for part in range(2)]
-        even = [split(a + b) for a, b in zip(near, far)]
-        odd = [split((b - a) * sign) for a, b in zip(near, far)]
-        u_new = dot3(*even[0], *c) + dot3(*odd[1], *s)
-        v_new = dot3(*even[1], *c) - dot3(*odd[0], *s)
-        u = u_new if u is None else u + u_new
-        v = v_new if v is None else v + v_new
-    lane = lax.broadcasted_iota(i32, (SUB, NX // 2), 1)
-    phase_cos, phase_sin = cos_sin_turn((lane * (NX - 1)) % (2 * NX), 2 * NX)
-    scale = 1.0 / math.sqrt(NX * NY)
-    phase_cos, phase_sin = phase_cos[0:1] * scale, phase_sin[0:1] * scale
-    out_ref[0] = u * phase_cos + v * phase_sin
-    out_ref[1] = v * phase_cos - u * phase_sin
-
-
-def make_x(late, tables, early):
-    half_size = len(early)
-    total = late[0].shape[0] // SUB - 1
+        return jnp.concatenate([ref[part, t] for t in range(blocks)], axis=1)
+
+    source = lax.bitwise_xor(narrow, mask)
+    mirror = 2 * half_size - 1 - source
+    sign = jnp.where(source < mirror, 1.0, -1.0).astype(f32)
+    start = pl.multiple_of((jnp.maximum(source, mirror) - half_size) * columns, columns)
+    cos_rows = pl.ds(start, columns)
+    sin_rows = pl.ds(pl.multiple_of(NX // 2 + start, columns), columns)
+    near = [whole(near_ref, part) for part in range(2)]
+    far = [whole(far_ref, part) for part in range(2)]
+    even = jnp.concatenate([a + b for a, b in zip(near, far)], axis=0)
+    odd = jnp.concatenate([(far[1] - near[1]) * sign, (near[0] - far[0]) * sign], axis=0)
+    even_high, even_low = split(even)
+    odd_high, odd_low = split(odd)
+    both = jnp.dot(
+        jnp.concatenate([even_high, even_low, even_high, odd_high, odd_low, odd_high], axis=1),
+        jnp.concatenate(
+            [
+                wx_high[cos_rows, :], wx_high[cos_rows, :], wx_low[cos_rows, :],
+                wx_high[sin_rows, :], wx_high[sin_rows, :], wx_low[sin_rows, :],
+            ],
+            axis=0,
+        ),
+        preferred_element_type=f32,
+    )
+    rows_all = wy_high.shape[0] // 2
+    u, v = both[:rows_all], both[rows_all:]
+    if not first:
+        u, v = u + sum_ref[0], v + sum_ref[1]
+    if last:
+        lane = lax.broadcasted_iota(i32, (SUB, NX // 2), 1)
+        phase_cos, phase_sin = cos_sin_turn((lane * (NX - 1)) % (2 * NX), 2 * NX)
+        scale = 1.0 / math.sqrt(NX * NY)
+        phase_cos, phase_sin = phase_cos[0:1] * scale, phase_sin[0:1] * scale
+        u, v = u * phase_cos + v * phase_sin, v * phase_cos - u * phase_sin
+    out_ref[0] = u
+    out_ref[1] = v
+
+
+def make_x(bricks, near, mask, tables, total, last, wide_size, slots):
+    first = total is None
     rows_all = tables[0].shape[0] // 2
-    columns = early[0].shape[1] * LANES
+    columns = near.shape[1] * LANES
     vmem = pl.BlockSpec(memory_space=pltpu.VMEM)
+    args = (bricks, near, *tables) if first else (bricks, near, *tables, total)
     return pl.pallas_call(
-        functools.partial(x_kernel, total, half_size),
-        in_specs=[vmem] * (4 + 2 * half_size),
+        functools.partial(x_kernel, slots, columns, mask, first, last),
+        in_specs=[vmem] * len(args),
         out_specs=vmem,
-        out_shape=jax.ShapeDtypeStruct((2, rows_all, NX // 2), f32),
-        scratch_shapes=[pltpu.VMEM((NY + BY, columns), f32), pltpu.SMEM((SUB, LANES), f32), pltpu.SemaphoreType.DMA]
-        + [pltpu.VMEM(early[0].shape, f32)] * half_size,
+        out_shape=(jax.ShapeDtypeStruct if last else pltpu.VMEM)((2, rows_all, NX // 2), f32),
+        scratch_shapes=[pltpu.VMEM(near.shape, f32)] + along_y_scratch(wide_size, columns),
+        compiler_params=pltpu.CompilerParams(vmem_limit_bytes=VMEM_LIMIT),
         name="along_x",
-    )(*late, *tables, *early)
+    )(*map(on_chip, args))
 
 
 def local(density_blocks, block_groups, block_brick, orbital_freq, orbital_phase, core_density):
@@ -474,7 +524,7 @@
     slots = (2 * block_count + wide_size - 1) // wide_size
     planes, grid_rows, columns = core_density.shape
     half_size = narrow_size // 2
-    assert narrow_size & (narrow_size - 1) == 0 and planes == 1 and slots <= SUB
+    assert narrow_size & (narrow_size - 1) == 0 and planes == 1 and slots <= LANES
     send = make_pieces(
         density_blocks, block_groups, block_brick, orbital_freq, orbital_phase, wide_size, slots, planes
     )
@@ -490,9 +540,14 @@
         bricks |= {mask | step: across(value, step) for mask, value in bricks.items()}
         step //= 2
     tables = make_tables(narrow_size)
-    early = [make_y(bricks[mask], tables, columns) for mask in range(half_size)]
-    late = [bricks[mask] for mask in range(half_size, narrow_size)]
-    return make_x(late, tables, early)[None]
+    early = [make_y(bricks[mask], tables, columns, wide_size, slots) for mask in range(half_size)]
+    total = None
+    for late in range(half_size, narrow_size):
+        mask = narrow_size - 1 - late
+        total = make_x(
+            bricks[late], early[mask], mask, tables, total, late == narrow_size - 1, wide_size, slots
+        )
+    return total[None]
 
 
 def solution(mesh):

time: 61 us -> 47.4 us (0.78)
  Pallas kernels: 40.2 us -> 27.2 us
  local copies, waits for them, and re-layouts: 1.35 us -> 0.01 us
  waiting for transfers between devices: 1.61 us -> 2.73 us
    pallas_call x3 -> x4, Pallas kernels: 17.5 us -> 9.26 us  [the longest x2 6.07 us: make_x(): pl.pallas_call(functools.partial(x_kernel, slots, columns, mask, first, l...]
    pallas_call x1, Pallas kernels: 5.35 us -> 2.56 us  [make_energy(): pl.pallas_call(functools.partial(energy_kernel, slots), in_specs=[vmem, v...]
    pallas_call x1, Pallas kernels: 2.84 us -> 1.47 us  [make_tables(): pl.pallas_call(tables_kernel, out_specs=[vmem] * 4, out_shape=[y_shape, y...]
    unnamed x6 -> x2, local copies, waits for them, and re-layouts: 1.35 us -> 0.01 us
    ppermute x3, waiting for transfers between devices: 1.61 us -> 2.73 us  [across(): lax.ppermute(value, 'narrow', [(i, i ^ mask) for i in range(narrow_size)])]
  transfers between devices with their start and end apart: 3 -> 3, of which waited for: 1 -> 1; matrix products, arithmetic and copies ran while one was open for 0% -> 0% of each run, Pallas kernels for 19% -> 15%
where the time goes in v2:
time: 47.4 us; the launch traced here: 47.1 us
  Pallas kernels  27.2 us (57%)
  blocking collectives  15.5 us (33%)
  waiting for transfers between devices  2.73 us (6%)
  starting transfers between devices  1.58 us (3%)
    all_to_all x1, blocking collectives, local(): got = lax.all_to_all(send, 'wide', split_axis=0, concat_axis=0, tiled=True)  15.5 us
    pallas_call x1, Pallas kernels, make_pieces(): pl.pallas_call(functools.partial(pieces_kernel, count, slots, planes), in...  13.9 us
    pallas_call x2, Pallas kernels, make_x(): pl.pallas_call(functools.partial(x_kernel, slots, columns, mask, first, l...  6.07 us
    pallas_call x2, Pallas kernels, make_y(): pl.pallas_call(functools.partial(y_kernel, slots, columns), in_specs=[vme...  3.19 us
    ppermute x3, waiting for transfers between devices, across(): lax.ppermute(value, 'narrow', [(i, i ^ mask) for i in range(narrow_size)])  2.73 us
    pallas_call x1, Pallas kernels, make_energy(): pl.pallas_call(functools.partial(energy_kernel, slots), in_specs=[vmem, v...  2.56 us
    ppermute x3, starting transfers between devices, across(): lax.ppermute(value, 'narrow', [(i, i ^ mask) for i in range(narrow_size)])  1.58 us
    pallas_call x1, Pallas kernels, make_tables(): pl.pallas_call(tables_kernel, out_specs=[vmem] * 4, out_shape=[y_shape, y...  1.47 us
  transfers between devices with their start and end apart: 3, of which 1 were waited for; matrix products, arithmetic and copies ran while one was open for 0% of the time, Pallas kernels for 15%

profile of v2, /device:TPU:0, one launch (start us, length us, event | category | flops | bytes accessed | tf_op | source)
XLA Modules:
  0.0 47.1 jit_solution(7704914194144478357)
XLA Ops:
  0.0 0.0 copy-start
  0.0 13.9 %pieces.1 = f32[8,56,128]{2,1,0:T(8,128)S(1)} custom-call(s32[2,24]{1,0:T(2,128)} %bitcast.4, s32[24]{0:T(128)} %brick_ref.1, f32[24,128,128]{2,1,0:T(8,128)} %blocks_ref.1, f32[3,8192]{1,0:T(4,128)} %freq_ref.1, f32[3,8192]{1,0:T(4,128)} %phase_ref.1), custom_call_target="tpu_custom_call" | custom-call | tf_op jit(solution)/shard_map/pieces/pallas_call | solution.py:218
  13.9 15.5 %all_to_all.5.got_ref = f32[8,56,128]{2,1,0:T(8,128)S(1)} all-to-all(f32[8,56,128]{2,1,0:T(8,128)S(1)} %pieces.1), channel_id=1, replica_groups=mesh['wide'=8,'narrow'=4] {'wide'}, dimensions={0} | all-to-all | bytes 458752 | tf_op jit(solution)/shard_map/all_to_all | solution.py:531
  29.5 0.0 copy-done
  29.5 2.6 %energy.1.bricks_ref = f32[392,128]{1,0:T(8,128)S(1)} custom-call(f32[8,56,128]{2,1,0:T(8,128)S(1)} %all_to_all.5.got_ref, f32[1024,256]{1,0:T(8,128)S(1)} %bitcast.3), custom_call_target="tpu_custom_call" | custom-call | tf_op jit(solution)/shard_map/energy/pallas_call | solution.py:311
  32.1 1.6 %collective-permute-start = (f32[392,128]{1,0:T(8,128)S(1)}, f32[392,128]{1,0:T(8,128)S(1)}, u32[]{:S(2)}, u32[]{:S(2)}) collective-permute-start(f32[392,128]{1,0:T(8,128)S(1)} %energy.1.bricks_ref), channel_id=1, source_target_pairs={{0,2},{1,3},{2,0},{3,1},{4,6},{5,7},{6,4},{7,5},{8,10},{9,11},{10,... | collective-permute-start | bytes 602120 | tf_op jit(solution)/shard_map/ppermute | solution.py:535
  33.6 0.0 collective-permute-start.2
  33.6 1.5 %tables.1 = (bf16[512,512]{1,0:T(8,128)(2,1)S(1)}, bf16[512,512]{1,0:T(8,128)(2,1)S(1)}, bf16[1024,512]{1,0:T(8,128)(2,1)S(1)}, bf16[1024,512]{1,0:T(8,128)(2,1)S(1)}) custom-call(), custom_call_target="tpu_custom_call" | custom-call | tf_op jit(solution)/shard_map/tables/pallas_call | solution.py:372
  35.1 2.7 %collective-permute-done.refs_0_ = f32[392,128]{1,0:T(8,128)S(1)} collective-permute-done((f32[392,128]{1,0:T(8,128)S(1)}, f32[392,128]{1,0:T(8,128)S(1)}, u32[]{:S(2)}, u32[]{:S(2)}) %collective-permute-start) | collective-permute-done | bytes 200736 | tf_op jit(solution)/shard_map/ppermute | solution.py:535
  37.8 0.0 collective-permute-start.1
  37.8 1.6 %along_y.2.refs_1_ = f32[2,2,256,128]{3,2,1,0:T(8,128)S(1)} custom-call(f32[392,128]{1,0:T(8,128)S(1)} %energy.1.bricks_ref, bf16[512,512]{1,0:T(8,128)(2,1)S(1)} %get-tuple-element.9.wy_high.refs_2_, bf16[512,512]{1,0:T(8,128)(2,1)S(1)} %get-tuple-element.10.wy_low.refs_3_), custom_call_target="tpu_custom_call" | custom-call | flops 2000000000 | bytes 2000000 | tf_op jit(solution)/shard_map/along_y/pallas_call | solution.py:441
  39.4 0.0 collective-permute-done.2.bricks_ref
  39.5 1.6 %along_y.3.refs_1_ = f32[2,2,256,128]{3,2,1,0:T(8,128)S(1)} custom-call(f32[392,128]{1,0:T(8,128)S(1)} %collective-permute-done.2.bricks_ref, bf16[512,512]{1,0:T(8,128)(2,1)S(1)} %get-tuple-element.9.wy_high.refs_2_, bf16[512,512]{1,0:T(8,128)(2,1)S(1)} %get-tuple-element.10.wy_low.refs_3_), custom_call_target="tpu_custom_call" | custom-call | flops 2000000000 | bytes 2000000 | tf_op jit(solution)/shard_map/along_y/pallas_call | solution.py:441
  41.1 2.5 %along_x.2.refs_6_ = f32[2,256,512]{2,1,0:T(8,128)S(1)} custom-call(f32[392,128]{1,0:T(8,128)S(1)} %collective-permute-done.refs_0_, f32[2,2,256,128]{3,2,1,0:T(8,128)S(1)} %along_y.3.refs_1_, bf16[512,512]{1,0:T(8,128)(2,1)S(1)} %get-tuple-element.9.wy_high.refs_2_, bf16[512,512]{1,0:T(8,128)(2,1)S(1)} %get-tuple-element.10.wy_low.refs_3_, ...), custom_call_target="tpu_custom_call" | custom-call | tf_op jit(solution)/shard_map/along_x/pallas_call | solution.py:509
  43.6 0.0 collective-permute-done.1.refs_0_
  43.6 3.6 %along_x.3 = f32[2,256,512]{2,1,0:T(8,128)} custom-call(f32[392,128]{1,0:T(8,128)S(1)} %collective-permute-done.1.refs_0_, f32[2,2,256,128]{3,2,1,0:T(8,128)S(1)} %along_y.2.refs_1_, bf16[512,512]{1,0:T(8,128)(2,1)S(1)} %get-tuple-element.9.wy_high.refs_2_, bf16[512,512]{1,0:T(8,128)(2,1)S(1)} %get-tuple-element.10.wy_low.refs_3_, ...), custom_call_target="tpu_custom_call" | custom-call | tf_op jit(solution)/shard_map/along_x/pallas_call | solution.py:509
Async XLA Ops:
  0.0 29.5 %copy-start = (f32[1,1024,256]{2,1,0:T(8,128)S(1)}, f32[1,1024,256]{2,1,0:T(8,128)}, u32[]{:S(2)}) copy-start(f32[1,1024,256]{2,1,0:T(8,128)} %param.11) | copy-start | bytes 3145732
  32.1 5.8 %collective-permute-start = (f32[392,128]{1,0:T(8,128)S(1)}, f32[392,128]{1,0:T(8,128)S(1)}, u32[]{:S(2)}, u32[]{:S(2)}) collective-permute-start(f32[392,128]{1,0:T(8,128)S(1)} %energy.1.bricks_ref), channel_id=1, source_target_pairs={{0,2},{1,3},{2,0},{3,1},{4,6},{5,7},{6,4},{7,5},{8,10},{9,11},{10,... | collective-permute-start | bytes 602120 | tf_op jit(solution)/shard_map/ppermute | solution.py:535
  33.6 5.8 %collective-permute-start.2 = (f32[392,128]{1,0:T(8,128)S(1)}, f32[392,128]{1,0:T(8,128)S(1)}, u32[]{:S(2)}, u32[]{:S(2)}) collective-permute-start(f32[392,128]{1,0:T(8,128)S(1)} %energy.1.bricks_ref), channel_id=1, source_target_pairs={{0,1},{1,0},{2,3},{3,2},{4,5},{5,4},{6,7},{7,6},{8,9},{9,8},{10,11... | collective-permute-start | bytes 602120 | tf_op jit(solution)/shard_map/ppermute | solution.py:535
  37.8 5.7 %collective-permute-start.1 = (f32[392,128]{1,0:T(8,128)S(1)}, f32[392,128]{1,0:T(8,128)S(1)}, u32[]{:S(2)}, u32[]{:S(2)}) collective-permute-start(f32[392,128]{1,0:T(8,128)S(1)} %collective-permute-done.refs_0_), channel_id=1, source_target_pairs={{0,1},{1,0},{2,3},{3,2},{4,5},{5,4},{6,7},{7,6},{8,9},{9,8},{10,11... | collective-permute-start | bytes 602120 | tf_op jit(solution)/shard_map/ppermute | solution.py:535

commit v3 on v2

--- a/solution.py
+++ b/solution.py
@@ -167,14 +167,13 @@
             odd = (lane & bit) != 0
             return jnp.where(odd, two, one) + pltpu.roll(jnp.where(odd, one, two), bit, 1)
 
-        sums = []
+        sums = jnp.zeros((SUB, LANES), f32)
         for part in range(PARTS):
-            sums.append(row_sums(part * (LANES // PARTS), LANES // PARTS))
+            for first in range(part * (LANES // PARTS), (part + 1) * (LANES // PARTS)):
+                cells = jnp.sum(row_sums(first, 1), axis=1, keepdims=True)
+                sums = jnp.where(lane == first, cells, sums)
             yield
-        while len(sums) > 1:
-            bit = LANES // len(sums)
-            sums = [merge(one, two, bit) for one, two in zip(sums[::2], sums[1::2])]
-        value = sums[0]
+        value = sums
         q = brick_ref[b]
         zb = q // (row_bricks * col_bricks)
         home = zb // planes

time: 47.4 us -> 43.6 us (0.920)
  Pallas kernels: 27.2 us -> 23.5 us
    pallas_call x1, Pallas kernels: 13.9 us -> 10.2 us  [make_pieces(): pl.pallas_call(functools.partial(pieces_kernel, count, slots, planes), in...]
  transfers between devices with their start and end apart: 3 -> 3, of which waited for: 1 -> 1; matrix products, arithmetic and copies ran while one was open for 0% -> 0% of each run, Pallas kernels for 15% -> 17%
where the time goes in v3:
time: 43.6 us; the launch traced here: 43.4 us
  Pallas kernels  23.5 us (54%)
  blocking collectives  15.5 us (36%)
  waiting for transfers between devices  2.73 us (6%)
  starting transfers between devices  1.58 us (4%)
    all_to_all x1, blocking collectives, local(): got = lax.all_to_all(send, 'wide', split_axis=0, concat_axis=0, tiled=True)  15.5 us
    pallas_call x1, Pallas kernels, make_pieces(): pl.pallas_call(functools.partial(pieces_kernel, count, slots, planes), in...  10.2 us
    pallas_call x2, Pallas kernels, make_x(): pl.pallas_call(functools.partial(x_kernel, slots, columns, mask, first, l...  6.07 us
    pallas_call x2, Pallas kernels, make_y(): pl.pallas_call(functools.partial(y_kernel, slots, columns), in_specs=[vme...  3.19 us
    ppermute x3, waiting for transfers between devices, across(): lax.ppermute(value, 'narrow', [(i, i ^ mask) for i in range(narrow_size)])  2.73 us
    pallas_call x1, Pallas kernels, make_energy(): pl.pallas_call(functools.partial(energy_kernel, slots), in_specs=[vmem, v...  2.57 us
    ppermute x3, starting transfers between devices, across(): lax.ppermute(value, 'narrow', [(i, i ^ mask) for i in range(narrow_size)])  1.58 us
    pallas_call x1, Pallas kernels, make_tables(): pl.pallas_call(tables_kernel, out_specs=[vmem] * 4, out_shape=[y_shape, y...  1.47 us
  transfers between devices with their start and end apart: 3, of which 1 were waited for; matrix products, arithmetic and copies ran while one was open for 0% of the time, Pallas kernels for 17%

profile of v3, /device:TPU:0, one launch (start us, length us, event | category | flops | bytes accessed | tf_op | source)
XLA Modules:
  0.0 43.4 jit_solution(16415846248864263700)
XLA Ops:
  0.0 0.0 copy-start
  0.0 10.2 %pieces.1 = f32[8,56,128]{2,1,0:T(8,128)S(1)} custom-call(s32[2,24]{1,0:T(2,128)} %bitcast.4, s32[24]{0:T(128)} %brick_ref.1, f32[24,128,128]{2,1,0:T(8,128)} %blocks_ref.1, f32[3,8192]{1,0:T(4,128)} %freq_ref.1, f32[3,8192]{1,0:T(4,128)} %phase_ref.1), custom_call_target="tpu_custom_call" | custom-call | tf_op jit(solution)/shard_map/pieces/pallas_call | solution.py:217
  10.2 15.5 %all_to_all.5.got_ref = f32[8,56,128]{2,1,0:T(8,128)S(1)} all-to-all(f32[8,56,128]{2,1,0:T(8,128)S(1)} %pieces.1), channel_id=1, replica_groups=mesh['wide'=8,'narrow'=4] {'wide'}, dimensions={0} | all-to-all | bytes 458752 | tf_op jit(solution)/shard_map/all_to_all | solution.py:530
  25.7 0.0 copy-done
  25.7 2.6 %energy.1.bricks_ref = f32[392,128]{1,0:T(8,128)S(1)} custom-call(f32[8,56,128]{2,1,0:T(8,128)S(1)} %all_to_all.5.got_ref, f32[1024,256]{1,0:T(8,128)S(1)} %bitcast.3), custom_call_target="tpu_custom_call" | custom-call | tf_op jit(solution)/shard_map/energy/pallas_call | solution.py:310
  28.3 1.6 %collective-permute-start = (f32[392,128]{1,0:T(8,128)S(1)}, f32[392,128]{1,0:T(8,128)S(1)}, u32[]{:S(2)}, u32[]{:S(2)}) collective-permute-start(f32[392,128]{1,0:T(8,128)S(1)} %energy.1.bricks_ref), channel_id=1, source_target_pairs={{0,2},{1,3},{2,0},{3,1},{4,6},{5,7},{6,4},{7,5},{8,10},{9,11},{10,... | collective-permute-start | bytes 602120 | tf_op jit(solution)/shard_map/ppermute | solution.py:534
  29.9 0.0 collective-permute-start.2
  29.9 1.5 %tables.1 = (bf16[512,512]{1,0:T(8,128)(2,1)S(1)}, bf16[512,512]{1,0:T(8,128)(2,1)S(1)}, bf16[1024,512]{1,0:T(8,128)(2,1)S(1)}, bf16[1024,512]{1,0:T(8,128)(2,1)S(1)}) custom-call(), custom_call_target="tpu_custom_call" | custom-call | tf_op jit(solution)/shard_map/tables/pallas_call | solution.py:371
  31.4 2.7 %collective-permute-done.refs_0_ = f32[392,128]{1,0:T(8,128)S(1)} collective-permute-done((f32[392,128]{1,0:T(8,128)S(1)}, f32[392,128]{1,0:T(8,128)S(1)}, u32[]{:S(2)}, u32[]{:S(2)}) %collective-permute-start) | collective-permute-done | bytes 200736 | tf_op jit(solution)/shard_map/ppermute | solution.py:534
  34.1 0.0 collective-permute-start.1
  34.1 1.6 %along_y.2.refs_1_ = f32[2,2,256,128]{3,2,1,0:T(8,128)S(1)} custom-call(f32[392,128]{1,0:T(8,128)S(1)} %energy.1.bricks_ref, bf16[512,512]{1,0:T(8,128)(2,1)S(1)} %get-tuple-element.9.wy_high.refs_2_, bf16[512,512]{1,0:T(8,128)(2,1)S(1)} %get-tuple-element.10.wy_low.refs_3_), custom_call_target="tpu_custom_call" | custom-call | flops 2000000000 | bytes 2000000 | tf_op jit(solution)/shard_map/along_y/pallas_call | solution.py:440
  35.7 0.0 collective-permute-done.2.bricks_ref
  35.7 1.6 %along_y.3.refs_1_ = f32[2,2,256,128]{3,2,1,0:T(8,128)S(1)} custom-call(f32[392,128]{1,0:T(8,128)S(1)} %collective-permute-done.2.bricks_ref, bf16[512,512]{1,0:T(8,128)(2,1)S(1)} %get-tuple-element.9.wy_high.refs_2_, bf16[512,512]{1,0:T(8,128)(2,1)S(1)} %get-tuple-element.10.wy_low.refs_3_), custom_call_target="tpu_custom_call" | custom-call | flops 2000000000 | bytes 2000000 | tf_op jit(solution)/shard_map/along_y/pallas_call | solution.py:440
  37.3 2.5 %along_x.2.refs_6_ = f32[2,256,512]{2,1,0:T(8,128)S(1)} custom-call(f32[392,128]{1,0:T(8,128)S(1)} %collective-permute-done.refs_0_, f32[2,2,256,128]{3,2,1,0:T(8,128)S(1)} %along_y.3.refs_1_, bf16[512,512]{1,0:T(8,128)(2,1)S(1)} %get-tuple-element.9.wy_high.refs_2_, bf16[512,512]{1,0:T(8,128)(2,1)S(1)} %get-tuple-element.10.wy_low.refs_3_, ...), custom_call_target="tpu_custom_call" | custom-call | tf_op jit(solution)/shard_map/along_x/pallas_call | solution.py:508
  39.9 0.0 collective-permute-done.1.refs_0_
  39.9 3.6 %along_x.3 = f32[2,256,512]{2,1,0:T(8,128)} custom-call(f32[392,128]{1,0:T(8,128)S(1)} %collective-permute-done.1.refs_0_, f32[2,2,256,128]{3,2,1,0:T(8,128)S(1)} %along_y.2.refs_1_, bf16[512,512]{1,0:T(8,128)(2,1)S(1)} %get-tuple-element.9.wy_high.refs_2_, bf16[512,512]{1,0:T(8,128)(2,1)S(1)} %get-tuple-element.10.wy_low.refs_3_, ...), custom_call_target="tpu_custom_call" | custom-call | tf_op jit(solution)/shard_map/along_x/pallas_call | solution.py:508
Async XLA Ops:
  0.0 25.7 %copy-start = (f32[1,1024,256]{2,1,0:T(8,128)S(1)}, f32[1,1024,256]{2,1,0:T(8,128)}, u32[]{:S(2)}) copy-start(f32[1,1024,256]{2,1,0:T(8,128)} %param.11) | copy-start | bytes 3145732
  28.3 5.8 %collective-permute-start = (f32[392,128]{1,0:T(8,128)S(1)}, f32[392,128]{1,0:T(8,128)S(1)}, u32[]{:S(2)}, u32[]{:S(2)}) collective-permute-start(f32[392,128]{1,0:T(8,128)S(1)} %energy.1.bricks_ref), channel_id=1, source_target_pairs={{0,2},{1,3},{2,0},{3,1},{4,6},{5,7},{6,4},{7,5},{8,10},{9,11},{10,... | collective-permute-start | bytes 602120 | tf_op jit(solution)/shard_map/ppermute | solution.py:534
  29.9 5.8 %collective-permute-start.2 = (f32[392,128]{1,0:T(8,128)S(1)}, f32[392,128]{1,0:T(8,128)S(1)}, u32[]{:S(2)}, u32[]{:S(2)}) collective-permute-start(f32[392,128]{1,0:T(8,128)S(1)} %energy.1.bricks_ref), channel_id=1, source_target_pairs={{0,1},{1,0},{2,3},{3,2},{4,5},{5,4},{6,7},{7,6},{8,9},{9,8},{10,11... | collective-permute-start | bytes 602120 | tf_op jit(solution)/shard_map/ppermute | solution.py:534
  34.1 5.7 %collective-permute-start.1 = (f32[392,128]{1,0:T(8,128)S(1)}, f32[392,128]{1,0:T(8,128)S(1)}, u32[]{:S(2)}, u32[]{:S(2)}) collective-permute-start(f32[392,128]{1,0:T(8,128)S(1)} %collective-permute-done.refs_0_), channel_id=1, source_target_pairs={{0,1},{1,0},{2,3},{3,2},{4,5},{5,4},{6,7},{7,6},{8,9},{9,8},{10,11... | collective-permute-start | bytes 602120 | tf_op jit(solution)/shard_map/ppermute | solution.py:534
